TPU v7x, 32 devices: a whole 2x2x4 slice. The times are simulated.
32 devices in a mesh: wide: 8 (over y, x, core), narrow: 4 (over z).
Axes of the slice: x: 2, y: 2, z: 4, core: 2. Of those that a mesh axis runs over, the one named last changes fastest.
Arguments:
- trajectory: bfloat16 [5, 72, 256, 1024], P(None, None, 'narrow', 'wide'), may hold values from -6 to 6
- innovation: float32 [5, 72, 64, 256], P(None, None, 'narrow', 'wide'), may hold values from -6 to 6
- background: float32 [5, 72, 64, 256], P(None, None, 'narrow', 'wide'), may hold values from -6 to 6
- obs_weight: float32 [72, 64, 256], P(None, 'narrow', 'wide'), may hold values from 0.3 to 3
Outputs:
- analysis: bfloat16 [5, 72, 256, 1024], P(None, None, 'narrow', 'wide')
All inputs are finite; a program needn't handle non-finite values.
Results may differ from a plain program's by a relative error of at most 0.001.
Values sent between devices are 32-bit elements; how exact they have to be, the bound alone decides.
A program may use at most 128 MiB of HBM per device.

v0:
```python
import jax
import jax.numpy as jnp
from jax import lax
from jax.sharding import PartitionSpec as P

FIELDS = 5
LEVELS = 72
COARSEN = 4
STEPS = 2


diffusion = 0.2
advection_scale = 0.3
descent_step = 1.0


def shifted(block, axis, distance):
    devices = range(lax.axis_size(axis))
    route = [((i - distance) % len(devices), i) for i in devices]
    return lax.ppermute(block, axis, route)


def from_behind(value, axis, steps):
    count = lax.axis_size(axis)
    first, last = (max(0, -steps), min(count, count - steps))
    return lax.ppermute(value, axis, [(source, source + steps) for source in range(first, last)])


def filter_rows(row_index, total_rows, cycle_size):
    wavenumber = jnp.arange(cycle_size, dtype=jnp.int32)
    folded = jnp.minimum(wavenumber, cycle_size - wavenumber).astype(jnp.float32)
    latitude = jnp.pi * ((row_index.astype(jnp.float32) + 0.5) / total_rows - 0.5)
    cutoff = 0.5 * cycle_size * jnp.cos(latitude)
    scaled_wave = folded[None, :] / cutoff[:, None]
    response = 1.0 / (1.0 + scaled_wave**4)
    phase_index = wavenumber[:, None] * wavenumber[None, :] % cycle_size
    angles = 2.0 * jnp.pi / cycle_size * phase_index.astype(jnp.float32)
    basis = jnp.concatenate([jnp.cos(angles), jnp.sin(angles)], axis=0)
    doubled = jnp.concatenate([response, response], axis=1)
    weighted = doubled[:, :, None] * basis[None]
    return jnp.einsum("rka,kb->rab", weighted, basis, precision=lax.Precision.HIGHEST) / cycle_size


def tangent_step(model_state, extend_rows, drift_coef, kernel):
    padded = extend_rows(model_state)
    north_row = padded[:, :, :-2]
    south_row = padded[:, :, 2:]
    east_cell = jnp.roll(model_state, -1, axis=3)
    west_cell = jnp.roll(model_state, 1, axis=3)
    updated = (
        model_state
        + diffusion * (north_row + south_row + east_cell + west_cell - 4.0 * model_state)
        + drift_coef * (east_cell - west_cell)
    )
    return jnp.einsum("flrb,rbc->flrc", updated, kernel, precision=lax.Precision.HIGHEST)


def adjoint_step(costate, extend_rows, drift_coef, kernel):
    filtered = jnp.einsum("flrb,rbc->flrc", costate, kernel, precision=lax.Precision.HIGHEST)
    padded = extend_rows(filtered)
    north_row = padded[:, :, :-2]
    south_row = padded[:, :, 2:]
    east_cell = jnp.roll(filtered, -1, axis=3)
    west_cell = jnp.roll(filtered, 1, axis=3)
    carried = drift_coef * filtered
    return (
        filtered
        + diffusion * (north_row + south_row + east_cell + west_cell - 4.0 * filtered)
        + jnp.roll(carried, 1, axis=3)
        - jnp.roll(carried, -1, axis=3)
    )


def shards(trajectory, innovation, background, obs_weight):
    wide_count = lax.axis_size("wide")
    narrow_count = lax.axis_size("narrow")
    wide_index = lax.axis_index("wide")
    narrow_index = lax.axis_index("narrow")
    coarse_rows = innovation.shape[2]
    coarse_cols = innovation.shape[3]
    fine_cols = trajectory.shape[3]
    total_rows = coarse_rows * narrow_count
    cycle_size = coarse_cols * wide_count
    zonal_wind = (
        trajectory[0]
        .astype(jnp.float32)
        .reshape(LEVELS, coarse_rows, COARSEN, fine_cols)
        .sum(axis=2)
    )
    zonal_wind = zonal_wind.reshape(LEVELS, coarse_rows, coarse_cols, COARSEN).sum(axis=3) / (
        COARSEN * COARSEN
    )
    side_fields = jnp.stack([obs_weight, advection_scale * jnp.tanh(zonal_wind)])
    band_rows = coarse_rows // wide_count
    level_count = LEVELS

    def spread(layer_field):
        return layer_field.reshape(layer_field.shape[0], LEVELS, wide_count, band_rows, coarse_cols)

    depart_part, backing_part, side_part = (
        lax.all_to_all(spread(innovation), "wide", split_axis=2, concat_axis=4, tiled=True),
        lax.all_to_all(spread(background), "wide", split_axis=2, concat_axis=4, tiled=True),
        lax.all_to_all(spread(side_fields), "wide", split_axis=2, concat_axis=4, tiled=True),
    )
    first_row = narrow_index * coarse_rows + wide_index * band_rows

    def extend_rows(model_state):
        upper_row = model_state[:, :, :1]
        lower_row = model_state[:, :, -1:]
        from_before = shifted(lower_row, "wide", 1)
        from_corner = from_behind(from_before, "narrow", 1)
        above_row = jnp.where(wide_index == 0, from_corner, from_before)
        from_after = shifted(upper_row, "wide", -1)
        from_beyond = from_behind(from_after, "narrow", -1)
        below_row = jnp.where(wide_index == wide_count - 1, from_beyond, from_after)
        return jnp.concatenate([above_row, model_state, below_row], axis=2)

    departure = depart_part.reshape(FIELDS, level_count, band_rows, cycle_size)
    backing = backing_part.reshape(FIELDS, level_count, band_rows, cycle_size)
    side_band = side_part.reshape(2, level_count, band_rows, cycle_size)
    weight_band = side_band[0][None]
    drift_coef = side_band[1][None]
    kernel = filter_rows(first_row + jnp.arange(band_rows, dtype=jnp.int32), total_rows, cycle_size)
    increment = backing
    model_state = increment
    for step_index in range(STEPS):
        model_state = tangent_step(model_state, extend_rows, drift_coef, kernel)
    costate = weight_band * (model_state - departure)
    for step_index in range(STEPS):
        costate = adjoint_step(costate, extend_rows, drift_coef, kernel)
    increment = increment - descent_step * (increment - backing + costate)
    moved_back = lax.all_to_all(
        increment.reshape(FIELDS, LEVELS, 1, band_rows, cycle_size),
        "wide",
        split_axis=4,
        concat_axis=2,
        tiled=True,
    )
    coarse_part = moved_back.reshape(FIELDS, LEVELS, coarse_rows, coarse_cols)
    fine_part = jnp.repeat(jnp.repeat(coarse_part, COARSEN, axis=3), COARSEN, axis=2)
    return (trajectory.astype(jnp.float32) + fine_part).astype(jnp.bfloat16)


def solution(mesh):
    in_specs = (
        P(None, None, "narrow", "wide"),
        P(None, None, "narrow", "wide"),
        P(None, None, "narrow", "wide"),
        P(None, "narrow", "wide"),
    )
    out_specs = P(None, None, "narrow", "wide")
    return jax.shard_map(shards, mesh=mesh, in_specs=in_specs, out_specs=out_specs, check_vma=False)
```

profile of v0, /device:TPU:0, one launch (start us, length us, event | category | flops | bytes accessed | tf_op | source)
XLA Modules:
  0.0 196.2 jit_solution(17924344261071722343)
XLA Ops:
  0.0 2.5 %copy.123 = f32[5,72,8,2,32]{1,4,3,0,2:T(8,128)} copy(f32[5,72,8,2,32]{1,4,3,2,0:T(8,128)} %bitcast.90) | data formatting | bytes 1474560 | tf_op jit(solution)/shard_map/reshape | solution.py:98
  2.5 5.2 %all-to-all-start = ((f32[5,72,8,2,32]{1,4,3,0,2:T(8,128)}), f32[5,72,8,2,32]{1,4,3,0,2:T(8,128)}, u32[]{:S(2)}, u32[]{:S(2)}) async-start(f32[5,72,8,2,32]{1,4,3,0,2:T(8,128)} %copy.123), calls=%async_computation | async-start | bytes 2621440 | tf_op jit(solution)/shard_map/all_to_all | solution.py:102
  7.7 1.0 fusion.47
  8.8 1.0 copy.127
  9.8 1.3 slice-done
  11.1 1.5 convert_reduce_fusion
  12.6 0.6 copy.128
  13.5 0.7 copy-done.6
  14.2 0.8 copy.130
  15.2 10.8 %all-to-all-done = f32[5,72,8,2,32]{1,4,3,0,2:T(8,128)} async-done(((f32[5,72,8,2,32]{1,4,3,0,2:T(8,128)}), f32[5,72,8,2,32]{1,4,3,0,2:T(8,128)}, u32[]{:S(2)}, u32[]{:S(2)}) %all-to-all-start) | async-done | bytes 737312 | tf_op jit(solution)/shard_map/all_to_all | solution.py:102
  26.0 4.1 %all-to-all-start.1 = ((f32[2,72,8,2,32]{1,4,3,0,2:T(8,128)}), f32[2,72,8,2,32]{1,4,3,0,2:T(8,128)}, u32[]{:S(2)}, u32[]{:S(2)}) async-start(f32[2,72,8,2,32]{1,4,3,0,2:T(8,128)} %copy.130), calls=%async_computation.1 | async-start | bytes 1048576 | tf_op jit(solution)/shard_map/all_to_all | solution.py:103
  30.2 1.4 copy.124
  31.7 0.4 copy.150
  32.0 0.9 fusion.68
  33.0 0.4 collective-permute-start
  33.4 1.0 convolution_multiply_fusion
  34.4 2.5 %copy.146 = f32[5,72,8,2,32]{1,4,3,0,2:T(8,128)} copy(f32[5,72,8,2,32]{1,4,3,2,0:T(8,128)} %bitcast.91) | data formatting | bytes 1474560 | tf_op jit(solution)/shard_map/reshape | solution.py:98
  36.9 2.3 %collective-permute-start.2 = (f32[5,72,1,256]{3,1,0,2:T(8,128)}, f32[5,72,1,256]{3,1,0,2:T(8,128)}, u32[]{:S(2)}, u32[]{:S(2)}) collective-permute-start(f32[5,72,1,256]{3,1,0,2:T(8,128)} %get-tuple-element.36), channel_id=1, source_target_pairs={{4,0},{8,4},{12,8},{16,12},{20,16},{24,20},{28,24},{0,28},{5,1},{9... | collective-permute-start | bytes 1105928 | tf_op jit(solution)/shard_map/ppermute | solution.py:20
  39.2 1.3 all-to-all-done.1
  40.5 3.6 %all-to-all-start.2 = ((f32[5,72,8,2,32]{1,4,3,0,2:T(8,128)}), f32[5,72,8,2,32]{1,4,3,0,2:T(8,128)S(1)}, u32[]{:S(2)}, u32[]{:S(2)}) async-start(f32[5,72,8,2,32]{1,4,3,0,2:T(8,128)} %copy.146), calls=%async_computation.2 | async-start | bytes 2621440 | tf_op jit(solution)/shard_map/all_to_all | solution.py:101
  44.0 1.8 fusion.69
  46.0 4.0 %collective-permute-start.1 = (f32[5,72,1,256]{3,1,0,2:T(8,128)}, f32[5,72,1,256]{3,1,0,2:T(8,128)S(1)}, u32[]{:S(2)}, u32[]{:S(2)}) collective-permute-start(f32[5,72,1,256]{3,1,0,2:T(8,128)} %collective-permute-done), channel_id=1, source_target_pairs={{0,1},{1,2},{2,3},{4,5},{5,6},{6,7},{8,9},{9,10},{10,11},{12,13},{... | collective-permute-start | bytes 1105928 | tf_op jit(solution)/shard_map/ppermute | solution.py:26
  50.2 1.3 collective-permute-start.3
  51.7 7.0 %collective-permute-done.1 = f32[5,72,1,256]{3,1,0,2:T(8,128)S(1)} collective-permute-done((f32[5,72,1,256]{3,1,0,2:T(8,128)}, f32[5,72,1,256]{3,1,0,2:T(8,128)S(1)}, u32[]{:S(2)}, u32[]{:S(2)}) %collective-permute-start.1) | collective-permute-done | bytes 368672 | tf_op jit(solution)/shard_map/ppermute | solution.py:26
  58.7 4.2 %collective-permute-done.3 = f32[5,72,1,256]{3,1,0,2:T(8,128)S(1)} collective-permute-done((f32[5,72,1,256]{3,1,0,2:T(8,128)}, f32[5,72,1,256]{3,1,0,2:T(8,128)S(1)}, u32[]{:S(2)}, u32[]{:S(2)}) %collective-permute-start.3) | collective-permute-done | bytes 368672 | tf_op jit(solution)/shard_map/ppermute | solution.py:26
  63.0 1.0 broadcast_select_fusion.3
  64.0 0.5 fusion.35
  64.5 0.8 fusion.70
  65.4 0.9 fusion.65
  66.3 2.6 %collective-permute-start.6 = (f32[5,72,1,256]{3,1,0,2:T(8,128)}, f32[5,72,1,256]{3,1,0,2:T(8,128)}, u32[]{:S(2)}, u32[]{:S(2)}) collective-permute-start(f32[5,72,1,256]{3,1,0,2:T(8,128)} %get-tuple-element.30), channel_id=1, source_target_pairs={{4,0},{8,4},{12,8},{16,12},{20,16},{24,20},{28,24},{0,28},{5,1},{9... | collective-permute-start | bytes 1105928 | tf_op jit(solution)/shard_map/ppermute | solution.py:20
  68.9 0.7 copy.131
  69.7 1.7 copy.132
  71.4 1.2 copy.147
  72.6 2.6 %copy.148 = f32[5,72,2,256]{3,1,2,0:T(8,128)} copy(f32[5,72,2,256]{1,3,2,0:T(8,128)} %bitcast.84) | data formatting | bytes 1474560 | tf_op jit(solution)/shard_map/reshape | solution.py:118
  75.2 1.3 collective-permute-done.4
  76.4 3.5 %collective-permute-start.5 = (f32[5,72,1,256]{3,1,0,2:T(8,128)}, f32[5,72,1,256]{3,1,0,2:T(8,128)S(1)}, u32[]{:S(2)}, u32[]{:S(2)}) collective-permute-start(f32[5,72,1,256]{3,1,0,2:T(8,128)} %collective-permute-done.4), channel_id=1, source_target_pairs={{0,1},{1,2},{2,3},{4,5},{5,6},{6,7},{8,9},{9,10},{10,11},{12,13},{... | collective-permute-start | bytes 1105928 | tf_op jit(solution)/shard_map/ppermute | solution.py:26
  80.2 1.5 collective-permute-start.7
  81.8 5.1 %collective-permute-done.5 = f32[5,72,1,256]{3,1,0,2:T(8,128)S(1)} collective-permute-done((f32[5,72,1,256]{3,1,0,2:T(8,128)}, f32[5,72,1,256]{3,1,0,2:T(8,128)S(1)}, u32[]{:S(2)}, u32[]{:S(2)}) %collective-permute-start.5) | collective-permute-done | bytes 368672 | tf_op jit(solution)/shard_map/ppermute | solution.py:26
  87.0 4.2 %collective-permute-done.7 = f32[5,72,1,256]{3,1,0,2:T(8,128)S(1)} collective-permute-done((f32[5,72,1,256]{3,1,0,2:T(8,128)}, f32[5,72,1,256]{3,1,0,2:T(8,128)S(1)}, u32[]{:S(2)}, u32[]{:S(2)}) %collective-permute-start.7) | collective-permute-done | bytes 368672 | tf_op jit(solution)/shard_map/ppermute | solution.py:26
  91.3 1.0 broadcast_select_fusion.2
  92.3 1.2 fusion.1
  93.6 0.8 fusion.71
  94.8 2.7 %collective-permute-start.10 = (f32[5,72,1,256]{3,1,0,2:T(8,128)S(1)}, f32[5,72,1,256]{3,1,0,2:T(8,128)S(1)}, u32[]{:S(2)}, u32[]{:S(2)}) collective-permute-start(f32[5,72,1,256]{3,1,0,2:T(8,128)S(1)} %get-tuple-element.24), channel_id=1, source_target_pairs={{4,0},{8,4},{12,8},{16,12},{20,16},{24,20},{28,24},{0,28},{5,1},{9... | collective-permute-start | bytes 1105928 | tf_op jit(solution)/shard_map/ppermute | solution.py:20
  97.8 8.1 %collective-permute-done.8 = f32[5,72,1,256]{3,1,0,2:T(8,128)S(1)} collective-permute-done((f32[5,72,1,256]{3,1,0,2:T(8,128)S(1)}, f32[5,72,1,256]{3,1,0,2:T(8,128)S(1)}, u32[]{:S(2)}, u32[]{:S(2)}) %collective-permute-start.8) | collective-permute-done | bytes 368672 | tf_op jit(solution)/shard_map/ppermute | solution.py:20
  105.8 3.5 %collective-permute-start.9 = (f32[5,72,1,256]{3,1,0,2:T(8,128)S(1)}, f32[5,72,1,256]{3,1,0,2:T(8,128)S(1)}, u32[]{:S(2)}, u32[]{:S(2)}) collective-permute-start(f32[5,72,1,256]{3,1,0,2:T(8,128)S(1)} %collective-permute-done.8), channel_id=1, source_target_pairs={{0,1},{1,2},{2,3},{4,5},{5,6},{6,7},{8,9},{9,10},{10,11},{12,13},{... | collective-permute-start | bytes 1105928 | tf_op jit(solution)/shard_map/ppermute | solution.py:26
  109.5 1.3 collective-permute-start.11
  111.0 4.8 %collective-permute-done.9 = f32[5,72,1,256]{3,1,0,2:T(8,128)S(1)} collective-permute-done((f32[5,72,1,256]{3,1,0,2:T(8,128)S(1)}, f32[5,72,1,256]{3,1,0,2:T(8,128)S(1)}, u32[]{:S(2)}, u32[]{:S(2)}) %collective-permute-start.9) | collective-permute-done | bytes 368672 | tf_op jit(solution)/shard_map/ppermute | solution.py:26
  115.9 4.3 %collective-permute-done.11 = f32[5,72,1,256]{3,1,0,2:T(8,128)S(1)} collective-permute-done((f32[5,72,1,256]{3,1,0,2:T(8,128)S(1)}, f32[5,72,1,256]{3,1,0,2:T(8,128)S(1)}, u32[]{:S(2)}, u32[]{:S(2)}) %collective-permute-start.11) | collective-permute-done | bytes 368672 | tf_op jit(solution)/shard_map/ppermute | solution.py:26
  120.2 0.7 fusion.21
  120.8 0.8 fusion.72
  122.1 2.7 %collective-permute-start.14 = (f32[5,72,1,256]{3,1,0,2:T(8,128)S(1)}, f32[5,72,1,256]{3,1,0,2:T(8,128)S(1)}, u32[]{:S(2)}, u32[]{:S(2)}) collective-permute-start(f32[5,72,1,256]{3,1,0,2:T(8,128)S(1)} %get-tuple-element.14), channel_id=1, source_target_pairs={{4,0},{8,4},{12,8},{16,12},{20,16},{24,20},{28,24},{0,28},{5,1},{9... | collective-permute-start | bytes 1105928 | tf_op jit(solution)/shard_map/ppermute | solution.py:20
  125.1 8.1 %collective-permute-done.12 = f32[5,72,1,256]{3,1,0,2:T(8,128)S(1)} collective-permute-done((f32[5,72,1,256]{3,1,0,2:T(8,128)S(1)}, f32[5,72,1,256]{3,1,0,2:T(8,128)S(1)}, u32[]{:S(2)}, u32[]{:S(2)}) %collective-permute-start.12) | collective-permute-done | bytes 368672 | tf_op jit(solution)/shard_map/ppermute | solution.py:20
  133.2 1.3 collective-permute-start.13
  134.6 1.3 collective-permute-start.15
  136.1 3.4 %collective-permute-done.13 = f32[5,72,1,256]{3,1,0,2:T(8,128)S(1)} collective-permute-done((f32[5,72,1,256]{3,1,0,2:T(8,128)S(1)}, f32[5,72,1,256]{3,1,0,2:T(8,128)S(1)}, u32[]{:S(2)}, u32[]{:S(2)}) %collective-permute-start.13) | collective-permute-done | bytes 368672 | tf_op jit(solution)/shard_map/ppermute | solution.py:26
  139.5 4.5 %collective-permute-done.15 = f32[5,72,1,256]{3,1,0,2:T(8,128)S(1)} collective-permute-done((f32[5,72,1,256]{3,1,0,2:T(8,128)S(1)}, f32[5,72,1,256]{3,1,0,2:T(8,128)S(1)}, u32[]{:S(2)}, u32[]{:S(2)}) %collective-permute-start.15) | collective-permute-done | bytes 368672 | tf_op jit(solution)/shard_map/ppermute | solution.py:26
  144.1 0.8 fusion.13
  144.9 0.9 copy.151
  145.8 21.9 %all_to_all.60 = f32[5,72,1,2,256]{1,3,2,0,4:T(2,128)S(1)} all-to-all(f32[5,72,1,2,256]{1,3,2,0,4:T(2,128)S(1)} %copy.151), channel_id=1, replica_groups=mesh['wide'=8,'narrow'=4] {'wide'}, dimensions={4} | all-to-all | bytes 1474560 | tf_op jit(solution)/shard_map/all_to_all | solution.py:132
  167.9 0.7 copy.154
  168.7 2.8 %broadcast_in_dim.4 = f32[5,72,16,32,4]{1,2,4,3,0:T(8,128)} broadcast(f32[5,72,16,32]{1,2,3,0:T(8,128)S(1)} %copy.154), dimensions={0,1,2,3} | broadcast | bytes 3686400 | tf_op jit(solution)/shard_map/broadcast_in_dim | solution.py:140
  171.4 5.5 %copy.155 = f32[5,72,16,128]{3,2,1,0:T(8,128)} copy(f32[5,72,16,128]{1,2,3,0:T(8,128)} %bitcast.80) | data formatting | bytes 5898240 | tf_op jit(solution)/shard_map/reshape | solution.py:140
  176.9 8.0 %broadcast_in_dim.5 = f32[5,72,16,4,128]{4,3,2,1,0:T(4,128)} broadcast(f32[5,72,16,128]{3,2,1,0:T(8,128)} %copy.155), dimensions={0,1,2,4} | broadcast | bytes 14745600 | tf_op jit(solution)/shard_map/broadcast_in_dim | solution.py:140
  185.0 11.2 %add_convert_fusion = bf16[5,72,64,128]{3,2,1,0:T(8,128)(2,1)} fusion(f32[5,72,64,128]{3,2,1,0:T(8,128)} %bitcast.65, bf16[5,72,64,128]{3,2,1,0:T(8,128)(2,1)} %param.4), kind=kLoop, calls=%fused_computation | loop fusion | flops 8847360 | bytes 23592960 | tf_op jit(solution)/shard_map/convert_element_type | solution.py:141
  (59 shorter events, 4.1 us)
Async XLA Ops:
  2.5 23.5 %all-to-all-start = ((f32[5,72,8,2,32]{1,4,3,0,2:T(8,128)}), f32[5,72,8,2,32]{1,4,3,0,2:T(8,128)}, u32[]{:S(2)}, u32[]{:S(2)}) async-start(f32[5,72,8,2,32]{1,4,3,0,2:T(8,128)} %copy.123), calls=%async_computation | async-start | bytes 2621440 | tf_op jit(solution)/shard_map/all_to_all | solution.py:102
  8.8 1.1 copy-start.1
  9.8 1.3 slice-start
  13.2 1.0 copy-start.6
  26.0 14.4 %all-to-all-start.1 = ((f32[2,72,8,2,32]{1,4,3,0,2:T(8,128)}), f32[2,72,8,2,32]{1,4,3,0,2:T(8,128)}, u32[]{:S(2)}, u32[]{:S(2)}) async-start(f32[2,72,8,2,32]{1,4,3,0,2:T(8,128)} %copy.130), calls=%async_computation.1 | async-start | bytes 1048576 | tf_op jit(solution)/shard_map/all_to_all | solution.py:103
  31.6 1.7 copy-start.2
  31.6 1.7 copy-start.3
  33.0 13.0 %collective-permute-start = (f32[5,72,1,256]{3,1,0,2:T(8,128)}, f32[5,72,1,256]{3,1,0,2:T(8,128)}, u32[]{:S(2)}, u32[]{:S(2)}) collective-permute-start(f32[5,72,1,256]{3,1,0,2:T(8,128)} %get-tuple-element.35), channel_id=1, source_target_pairs={{28,0},{0,4},{4,8},{8,12},{12,16},{16,20},{20,24},{24,28},{29,1},{... | collective-permute-start | bytes 1105928 | tf_op jit(solution)/shard_map/ppermute | solution.py:20
  36.9 13.3 %collective-permute-start.2 = (f32[5,72,1,256]{3,1,0,2:T(8,128)}, f32[5,72,1,256]{3,1,0,2:T(8,128)}, u32[]{:S(2)}, u32[]{:S(2)}) collective-permute-start(f32[5,72,1,256]{3,1,0,2:T(8,128)} %get-tuple-element.36), channel_id=1, source_target_pairs={{4,0},{8,4},{12,8},{16,12},{20,16},{24,20},{28,24},{0,28},{5,1},{9... | collective-permute-start | bytes 1105928 | tf_op jit(solution)/shard_map/ppermute | solution.py:20
  40.5 30.9 %all-to-all-start.2 = ((f32[5,72,8,2,32]{1,4,3,0,2:T(8,128)}), f32[5,72,8,2,32]{1,4,3,0,2:T(8,128)S(1)}, u32[]{:S(2)}, u32[]{:S(2)}) async-start(f32[5,72,8,2,32]{1,4,3,0,2:T(8,128)} %copy.146), calls=%async_computation.2 | async-start | bytes 2621440 | tf_op jit(solution)/shard_map/all_to_all | solution.py:101
  46.0 12.6 %collective-permute-start.1 = (f32[5,72,1,256]{3,1,0,2:T(8,128)}, f32[5,72,1,256]{3,1,0,2:T(8,128)S(1)}, u32[]{:S(2)}, u32[]{:S(2)}) collective-permute-start(f32[5,72,1,256]{3,1,0,2:T(8,128)} %collective-permute-done), channel_id=1, source_target_pairs={{0,1},{1,2},{2,3},{4,5},{5,6},{6,7},{8,9},{9,10},{10,11},{12,13},{... | collective-permute-start | bytes 1105928 | tf_op jit(solution)/shard_map/ppermute | solution.py:26
  50.2 12.7 %collective-permute-start.3 = (f32[5,72,1,256]{3,1,0,2:T(8,128)}, f32[5,72,1,256]{3,1,0,2:T(8,128)S(1)}, u32[]{:S(2)}, u32[]{:S(2)}) collective-permute-start(f32[5,72,1,256]{3,1,0,2:T(8,128)} %collective-permute-done.2), channel_id=1, source_target_pairs={{1,0},{2,1},{3,2},{5,4},{6,5},{7,6},{9,8},{10,9},{11,10},{13,12},{... | collective-permute-start | bytes 1105928 | tf_op jit(solution)/shard_map/ppermute | solution.py:26
  64.5 4.4 %copy-start.4 = (f32[1,72,1,2,8,32]{1,5,3,0,4,2:T(8,128)S(1)}, f32[1,72,1,2,8,32]{1,5,3,0,4,2:T(8,128)}, u32[]{:S(2)}) copy-start(f32[1,72,1,2,8,32]{1,5,3,0,4,2:T(8,128)} %get-tuple-element.37) | copy-start | bytes 442372
  66.3 10.1 %collective-permute-start.4 = (f32[5,72,1,256]{3,1,0,2:T(8,128)}, f32[5,72,1,256]{3,1,0,2:T(8,128)}, u32[]{:S(2)}, u32[]{:S(2)}) collective-permute-start(f32[5,72,1,256]{3,1,0,2:T(8,128)} %get-tuple-element.29), channel_id=1, source_target_pairs={{28,0},{0,4},{4,8},{8,12},{12,16},{16,20},{20,24},{24,28},{29,1},{... | collective-permute-start | bytes 1105928 | tf_op jit(solution)/shard_map/ppermute | solution.py:20
  66.3 13.9 %collective-permute-start.6 = (f32[5,72,1,256]{3,1,0,2:T(8,128)}, f32[5,72,1,256]{3,1,0,2:T(8,128)}, u32[]{:S(2)}, u32[]{:S(2)}) collective-permute-start(f32[5,72,1,256]{3,1,0,2:T(8,128)} %get-tuple-element.30), channel_id=1, source_target_pairs={{4,0},{8,4},{12,8},{16,12},{20,16},{24,20},{28,24},{0,28},{5,1},{9... | collective-permute-start | bytes 1105928 | tf_op jit(solution)/shard_map/ppermute | solution.py:20
  76.4 10.5 %collective-permute-start.5 = (f32[5,72,1,256]{3,1,0,2:T(8,128)}, f32[5,72,1,256]{3,1,0,2:T(8,128)S(1)}, u32[]{:S(2)}, u32[]{:S(2)}) collective-permute-start(f32[5,72,1,256]{3,1,0,2:T(8,128)} %collective-permute-done.4), channel_id=1, source_target_pairs={{0,1},{1,2},{2,3},{4,5},{5,6},{6,7},{8,9},{9,10},{10,11},{12,13},{... | collective-permute-start | bytes 1105928 | tf_op jit(solution)/shard_map/ppermute | solution.py:26
  80.2 11.1 %collective-permute-start.7 = (f32[5,72,1,256]{3,1,0,2:T(8,128)}, f32[5,72,1,256]{3,1,0,2:T(8,128)S(1)}, u32[]{:S(2)}, u32[]{:S(2)}) collective-permute-start(f32[5,72,1,256]{3,1,0,2:T(8,128)} %collective-permute-done.6), channel_id=1, source_target_pairs={{1,0},{2,1},{3,2},{5,4},{6,5},{7,6},{9,8},{10,9},{11,10},{13,12},{... | collective-permute-start | bytes 1105928 | tf_op jit(solution)/shard_map/ppermute | solution.py:26
  81.8 10.5 %copy-start = (f32[5,72,2,256]{3,1,2,0:T(8,128)S(1)}, f32[5,72,2,256]{3,1,2,0:T(8,128)}, u32[]{:S(2)}) copy-start(f32[5,72,2,256]{3,1,2,0:T(8,128)} %copy.148) | copy-start | bytes 2211844
  81.8 10.5 %copy-start.5 = (f32[72,2,256]{2,0,1:T(8,128)S(1)}, f32[72,2,256]{2,0,1:T(8,128)}, u32[]{:S(2)}) copy-start(f32[72,2,256]{2,0,1:T(8,128)} %copy.132) | copy-start | bytes 442372
  94.7 11.1 %collective-permute-start.8 = (f32[5,72,1,256]{3,1,0,2:T(8,128)S(1)}, f32[5,72,1,256]{3,1,0,2:T(8,128)S(1)}, u32[]{:S(2)}, u32[]{:S(2)}) collective-permute-start(f32[5,72,1,256]{3,1,0,2:T(8,128)S(1)} %get-tuple-element.23), channel_id=1, source_target_pairs={{28,0},{0,4},{4,8},{8,12},{12,16},{16,20},{20,24},{24,28},{29,1},{... | collective-permute-start | bytes 1105928 | tf_op jit(solution)/shard_map/ppermute | solution.py:20
  94.8 14.7 %collective-permute-start.10 = (f32[5,72,1,256]{3,1,0,2:T(8,128)S(1)}, f32[5,72,1,256]{3,1,0,2:T(8,128)S(1)}, u32[]{:S(2)}, u32[]{:S(2)}) collective-permute-start(f32[5,72,1,256]{3,1,0,2:T(8,128)S(1)} %get-tuple-element.24), channel_id=1, source_target_pairs={{4,0},{8,4},{12,8},{16,12},{20,16},{24,20},{28,24},{0,28},{5,1},{9... | collective-permute-start | bytes 1105928 | tf_op jit(solution)/shard_map/ppermute | solution.py:20
  105.8 10.0 %collective-permute-start.9 = (f32[5,72,1,256]{3,1,0,2:T(8,128)S(1)}, f32[5,72,1,256]{3,1,0,2:T(8,128)S(1)}, u32[]{:S(2)}, u32[]{:S(2)}) collective-permute-start(f32[5,72,1,256]{3,1,0,2:T(8,128)S(1)} %collective-permute-done.8), channel_id=1, source_target_pairs={{0,1},{1,2},{2,3},{4,5},{5,6},{6,7},{8,9},{9,10},{10,11},{12,13},{... | collective-permute-start | bytes 1105928 | tf_op jit(solution)/shard_map/ppermute | solution.py:26
  109.5 10.6 %collective-permute-start.11 = (f32[5,72,1,256]{3,1,0,2:T(8,128)S(1)}, f32[5,72,1,256]{3,1,0,2:T(8,128)S(1)}, u32[]{:S(2)}, u32[]{:S(2)}) collective-permute-start(f32[5,72,1,256]{3,1,0,2:T(8,128)S(1)} %collective-permute-done.10), channel_id=1, source_target_pairs={{1,0},{2,1},{3,2},{5,4},{6,5},{7,6},{9,8},{10,9},{11,10},{13,12},{... | collective-permute-start | bytes 1105928 | tf_op jit(solution)/shard_map/ppermute | solution.py:26
  122.0 11.2 %collective-permute-start.12 = (f32[5,72,1,256]{3,1,0,2:T(8,128)S(1)}, f32[5,72,1,256]{3,1,0,2:T(8,128)S(1)}, u32[]{:S(2)}, u32[]{:S(2)}) collective-permute-start(f32[5,72,1,256]{3,1,0,2:T(8,128)S(1)} %get-tuple-element.13), channel_id=1, source_target_pairs={{28,0},{0,4},{4,8},{8,12},{12,16},{16,20},{20,24},{24,28},{29,1},{... | collective-permute-start | bytes 1105928 | tf_op jit(solution)/shard_map/ppermute | solution.py:20
  122.1 12.5 %collective-permute-start.14 = (f32[5,72,1,256]{3,1,0,2:T(8,128)S(1)}, f32[5,72,1,256]{3,1,0,2:T(8,128)S(1)}, u32[]{:S(2)}, u32[]{:S(2)}) collective-permute-start(f32[5,72,1,256]{3,1,0,2:T(8,128)S(1)} %get-tuple-element.14), channel_id=1, source_target_pairs={{4,0},{8,4},{12,8},{16,12},{20,16},{24,20},{28,24},{0,28},{5,1},{9... | collective-permute-start | bytes 1105928 | tf_op jit(solution)/shard_map/ppermute | solution.py:20
  133.2 6.3 %collective-permute-start.13 = (f32[5,72,1,256]{3,1,0,2:T(8,128)S(1)}, f32[5,72,1,256]{3,1,0,2:T(8,128)S(1)}, u32[]{:S(2)}, u32[]{:S(2)}) collective-permute-start(f32[5,72,1,256]{3,1,0,2:T(8,128)S(1)} %collective-permute-done.12), channel_id=1, source_target_pairs={{0,1},{1,2},{2,3},{4,5},{5,6},{6,7},{8,9},{9,10},{10,11},{12,13},{... | collective-permute-start | bytes 1105928 | tf_op jit(solution)/shard_map/ppermute | solution.py:26
  134.6 9.4 %collective-permute-start.15 = (f32[5,72,1,256]{3,1,0,2:T(8,128)S(1)}, f32[5,72,1,256]{3,1,0,2:T(8,128)S(1)}, u32[]{:S(2)}, u32[]{:S(2)}) collective-permute-start(f32[5,72,1,256]{3,1,0,2:T(8,128)S(1)} %collective-permute-done.14), channel_id=1, source_target_pairs={{1,0},{2,1},{3,2},{5,4},{6,5},{7,6},{9,8},{10,9},{11,10},{13,12},{... | collective-permute-start | bytes 1105928 | tf_op jit(solution)/shard_map/ppermute | solution.py:26
where the time goes:
time: 197 us; the launch traced here: 196 us
  waiting for transfers between devices  67.1 us (34%)
  local copies, waits for them, and re-layouts  42.3 us (21%)
  starting transfers between devices  41.2 us (21%)
  blocking collectives  21.9 us (11%)
  other arithmetic  18.7 us (9%)
  matrix products  4.62 us (2%)
    ppermute x8, waiting for transfers between devices, from_behind(): lax.ppermute(value, axis, [(source, source + steps) for source in range(f...  37.6 us
    all_to_all x1, blocking collectives, shards(): lax.all_to_all(increment.reshape(FIELDS, LEVELS, 1, band_rows, cycle_size...  21.9 us
    ppermute x8, starting transfers between devices, from_behind(): lax.ppermute(value, axis, [(source, source + steps) for source in range(f...  17.6 us
    ppermute x8, waiting for transfers between devices, shifted(): return lax.ppermute(block, axis, route)  17.5 us
    convert_element_type x1, other arithmetic, shards(): return (trajectory.astype(jnp.float32) + fine_part).astype(jnp.bfloat16)  11.2 us
    all_to_all x1, waiting for transfers between devices, shards(): lax.all_to_all(spread(background), 'wide', split_axis=2, concat_axis=4, t...  10.8 us
    ppermute x8, starting transfers between devices, shifted(): return lax.ppermute(block, axis, route)  10.8 us
    broadcast_in_dim x1, local copies, waits for them, and re-layouts, shards(): jnp.repeat(jnp.repeat(coarse_part, COARSEN, axis=3), COARSEN, axis=2)  8.05 us
  transfers between devices with their start and end apart: 19, of which 13 were waited for; matrix products, arithmetic and copies ran while one was open for 13% of the time, Pallas kernels for 0%

commit v1 on v0

v1 whole, which is shorter than its diff:
```python
import functools

import jax
import jax.numpy as jnp
import numpy as np
from jax import lax
from jax.experimental import pallas as pl
from jax.experimental.pallas import tpu as pltpu
from jax.sharding import PartitionSpec as P

MESH = pl.DeviceIdType.MESH
FIELDS = 5
COARSEN = 4
STEPS = 2
LANES = 128
HALO = 2 * STEPS
ITEMS = 2 * FIELDS + 2

diffusion = 0.2
advection_scale = 0.3
descent_step = 1.0


def split_bf16(x):
    high = x.astype(jnp.bfloat16)
    low = (x - high.astype(jnp.float32)).astype(jnp.bfloat16)
    return high, low


def dot(a, b):
    return jnp.dot(a, b, preferred_element_type=jnp.float32)


def block_transpose(tiles, block):
    lane = lax.broadcasted_iota(jnp.int32, tiles[0].shape, len(tiles[0].shape) - 1) // block
    axis = len(tiles[0].shape) - 1
    tiles = list(tiles)
    for step in (2, 1):
        upper = (lane // step) % 2 == 1
        for first in range(4):
            if (first // step) % 2 == 0:
                second = first + step
                a, b = tiles[first], tiles[second]
                tiles[first] = jnp.where(upper, pltpu.roll(b, step * block, axis), a)
                tiles[second] = jnp.where(upper, b, pltpu.roll(a, LANES - step * block, axis))
    return tiles


def pack_kernel(traj_ref, depart_ref, back_ref, weight_ref, pool_ref, out_ref, sums):
    levels, fine_rows, fine_cols = traj_ref.shape[1:]
    rows = fine_rows // COARSEN
    cols = fine_cols // COARSEN
    sums[...] = dot(traj_ref[0].reshape(levels * fine_rows, fine_cols), pool_ref[...])
    total = sums[pl.ds(0, levels * rows, stride=COARSEN), :]
    for t in range(1, COARSEN):
        total = total + sums[pl.ds(t, levels * rows, stride=COARSEN), :]
    drift = advection_scale * jnp.tanh(total * (1.0 / (COARSEN * COARSEN)))
    drift = drift[:, :cols].reshape(levels, rows, cols)
    items = [back_ref[f] for f in range(FIELDS)] + [drift, weight_ref[...]]
    items += [depart_ref[f] for f in range(FIELDS)]
    for group in range(ITEMS // 4):
        out_ref[:, group] = jnp.concatenate(items[4 * group : 4 * group + 4], axis=-1)


def stencil(q, drift):
    rows, cycle = q.shape[-2:]
    north = pltpu.roll(q, 1, q.ndim - 2)
    south = pltpu.roll(q, rows - 1, q.ndim - 2)
    east = pltpu.roll(q, cycle - 1, q.ndim - 1)
    west = pltpu.roll(q, 1, q.ndim - 1)
    return q + diffusion * (north + south + east + west - 4.0 * q) + drift * (east - west)


def stencil_transposed(g, drift):
    rows, cycle = g.shape[-2:]
    north = pltpu.roll(g, 1, g.ndim - 2)
    south = pltpu.roll(g, rows - 1, g.ndim - 2)
    east = pltpu.roll(g, cycle - 1, g.ndim - 1)
    west = pltpu.roll(g, 1, g.ndim - 1)
    carried = drift * g
    return (
        g
        + diffusion * (north + south + east + west - 4.0 * g)
        + pltpu.roll(carried, 1, g.ndim - 1)
        - pltpu.roll(carried, cycle - 1, g.ndim - 1)
    )


def sweep_kernel(
    wide_count, narrow_count, levels, chunk,
    x_ref, response_ref, wave_high_ref, wave_low_ref, out_ref,
    landed, fields, result, outgoing, up_out, down_out, up_in, down_in,
    local_sem, send_sem, recv_sem, halo_send, halo_recv, back_send, back_recv,
):
    me = lax.axis_index("wide")
    band = lax.axis_index("narrow")
    has_above = band > 0
    has_below = band < narrow_count - 1
    rows = landed.shape[2]
    cycle = fields.shape[2]
    half = cycle // 2
    cols = cycle // wide_count
    padded = fields.shape[1]
    groups = out_ref.shape[1]

    barrier = pltpu.get_barrier_semaphore()
    for k in range(1, wide_count):
        pl.semaphore_signal(
            barrier, inc=1, device_id=(lax.rem(me + k, wide_count), band), device_id_type=MESH
        )

    @pl.when(has_above)
    def _():
        pl.semaphore_signal(barrier, inc=1, device_id=(me, band - 1), device_id_type=MESH)

    @pl.when(has_below)
    def _():
        pl.semaphore_signal(barrier, inc=1, device_id=(me, band + 1), device_id_type=MESH)

    keep = pltpu.make_async_copy(x_ref.at[me], landed.at[me], local_sem.at[0])
    keep.start()
    neighbours = has_above.astype(jnp.int32) + has_below.astype(jnp.int32)
    pl.semaphore_wait(barrier, wide_count - 1 + neighbours)

    sends = []
    for k in range(1, wide_count):
        peer = lax.rem(me + k, wide_count)
        copy = pltpu.make_async_remote_copy(
            src_ref=x_ref.at[peer],
            dst_ref=landed.at[me],
            send_sem=send_sem.at[k],
            recv_sem=recv_sem.at[k],
            device_id=(peer, band),
            device_id_type=MESH,
        )
        copy.start()
        sends.append(copy)
    keep.wait()
    for copy in sends:
        copy.wait_recv()

    low_half = lax.broadcasted_iota(jnp.int32, (8, half), 0) < HALO

    def unpack(level, carry):
        for group in range(ITEMS // 4):
            for tile in range(cycle // LANES):
                got = [landed[4 * tile + m, level * (ITEMS // 4) + group] for m in range(4)]
                for j, value in enumerate(block_transpose(got, cols)):
                    fields[level * ITEMS + 4 * group + j, 0:rows, tile * LANES : (tile + 1) * LANES] = value
        for item in range(ITEMS):
            at = level * ITEMS + item
            top = fields[at, 0:8]
            bottom = fields[at, rows - 8 : rows]
            up_out[at] = jnp.where(low_half, top[:, :half], pltpu.roll(top[:, half:], HALO, 0))
            down_out[at] = jnp.where(low_half, pltpu.roll(bottom[:, :half], HALO, 0), bottom[:, half:])
        return carry

    lax.fori_loop(0, levels, unpack, 0)

    up_copy = pltpu.make_async_remote_copy(
        src_ref=up_out, dst_ref=up_in, send_sem=halo_send.at[0], recv_sem=halo_recv.at[0],
        device_id=(me, band - 1), device_id_type=MESH,
    )
    down_copy = pltpu.make_async_remote_copy(
        src_ref=down_out, dst_ref=down_in, send_sem=halo_send.at[1], recv_sem=halo_recv.at[1],
        device_id=(me, band + 1), device_id_type=MESH,
    )

    @pl.when(has_above)
    def _():
        up_copy.start()

    @pl.when(has_below)
    def _():
        down_copy.start()

    @pl.when(jnp.logical_not(has_below))
    def _():
        up_in[...] = jnp.zeros_like(up_in)

    @pl.when(jnp.logical_not(has_above))
    def _():
        down_in[...] = jnp.zeros_like(down_in)

    @pl.when(has_below)
    def _():
        up_copy.wait_recv()

    @pl.when(has_above)
    def _():
        down_copy.wait_recv()

    def take_halo(level, carry):
        for item in range(ITEMS):
            at = level * ITEMS + item
            below, above = up_in[at], down_in[at]
            fields[at, rows:padded, 0:half] = jnp.where(low_half, below, pltpu.roll(above, HALO, 0))
            fields[at, rows:padded, half:cycle] = jnp.where(low_half, pltpu.roll(below, HALO, 0), above)
        return carry

    lax.fori_loop(0, levels, take_halo, 0)

    def zonal(q):
        shape = q.shape
        high, low = split_bf16(q.reshape(-1, cycle))
        wave_high, wave_low = wave_high_ref[...], wave_low_ref[...]
        spectrum = dot(high, wave_high) + dot(low, wave_high) + dot(high, wave_low)
        spectrum = spectrum.reshape(shape) * response_ref[...]
        high, low = split_bf16(spectrum.reshape(-1, cycle))
        return (dot(high, wave_high) + dot(low, wave_high) + dot(high, wave_low)).reshape(shape)

    def sweep(turn, carry):
        at = turn * chunk
        block = fields[pl.ds(at * ITEMS, chunk * ITEMS)].reshape(chunk, ITEMS, padded, cycle)
        background = block[:, :FIELDS]
        drift = block[:, FIELDS : FIELDS + 1]
        weight = block[:, FIELDS + 1 : FIELDS + 2]
        departure = block[:, FIELDS + 2 :]
        state = background
        for _ in range(STEPS):
            state = zonal(stencil(state, drift))
        costate = weight * (state - departure)
        for _ in range(STEPS):
            costate = stencil_transposed(zonal(costate), drift)
        increment = background - descent_step * ((background - background) + costate)
        result[pl.ds(at * FIELDS, chunk * FIELDS)] = increment.reshape(chunk * FIELDS, padded, cycle)[:, :rows]
        return carry

    lax.fori_loop(0, levels // chunk, sweep, 0)

    def repack(group, carry):
        for tile in range(cycle // LANES):
            parts = [result[4 * group + j, :, tile * LANES : (tile + 1) * LANES] for j in range(4)]
            for m, value in enumerate(block_transpose(parts, cols)):
                outgoing[4 * tile + m, group] = value
        return carry

    lax.fori_loop(0, groups, repack, 0)

    keep_back = pltpu.make_async_copy(outgoing.at[me], out_ref.at[me], local_sem.at[1])
    keep_back.start()
    backs = []
    for k in range(1, wide_count):
        peer = lax.rem(me + k, wide_count)
        copy = pltpu.make_async_remote_copy(
            src_ref=outgoing.at[peer],
            dst_ref=out_ref.at[me],
            send_sem=back_send.at[k],
            recv_sem=back_recv.at[k],
            device_id=(peer, band),
            device_id_type=MESH,
        )
        copy.start()
        backs.append(copy)
    for copy in sends:
        copy.wait_send()

    @pl.when(has_above)
    def _():
        up_copy.wait_send()

    @pl.when(has_below)
    def _():
        down_copy.wait_send()

    keep_back.wait()
    for copy in backs:
        copy.wait()


def finish_kernel(traj_ref, inc_ref, spread_ref, out_ref, wide, tall):
    fields, levels, fine_rows, fine_cols = traj_ref.shape
    groups, rows = inc_ref.shape[1:3]
    high, low = split_bf16(inc_ref[0].reshape(groups * rows, LANES))
    wide[...] = dot(high, spread_ref[...]) + dot(low, spread_ref[...])
    for level in range(levels):
        for f in range(fields):
            item = level * fields + f
            group, j = divmod(item, 4)
            part = wide[group * rows : (group + 1) * rows, j * LANES : (j + 1) * LANES]
            for t in range(COARSEN):
                tall[item, pl.ds(t, rows, stride=COARSEN), :] = part
            out_ref[f, level] = (traj_ref[f, level].astype(jnp.float32) + tall[item]).astype(jnp.bfloat16)


def shards(trajectory, innovation, background, obs_weight):
    wide_count = lax.axis_size("wide")
    narrow_count = lax.axis_size("narrow")
    narrow_index = lax.axis_index("narrow")
    fields, total_levels, rows, cols = innovation.shape
    fine_rows, fine_cols = trajectory.shape[2:]
    cycle = cols * wide_count
    total_rows = rows * narrow_count
    levels = -(-total_levels // wide_count)
    last = -(-total_levels // levels) - 1
    chunk = max(c for c in range(1, 6) if levels % c == 0)
    packed = ITEMS // 4
    groups = -(-fields * levels // 4)
    padded = rows + 2 * HALO

    lane = np.arange(fine_cols)
    pool = np.zeros((fine_cols, LANES), np.float32)
    pool[lane, lane // COARSEN] = 1.0
    spread = np.zeros((LANES, 4 * LANES), np.float32)
    for j in range(4):
        spread[j * cols + lane // COARSEN, j * LANES + lane] = 1.0
    pool = jnp.asarray(pool, jnp.bfloat16)
    spread = jnp.asarray(spread, jnp.bfloat16)

    sent = pl.pallas_call(
        pack_kernel,
        grid=(wide_count,),
        in_specs=[
            pl.BlockSpec((1, levels, fine_rows, fine_cols), lambda s: (0, jnp.minimum(s, last), 0, 0)),
            pl.BlockSpec((fields, levels, rows, cols), lambda s: (0, jnp.minimum(s, last), 0, 0)),
            pl.BlockSpec((fields, levels, rows, cols), lambda s: (0, jnp.minimum(s, last), 0, 0)),
            pl.BlockSpec((levels, rows, cols), lambda s: (jnp.minimum(s, last), 0, 0)),
            pl.BlockSpec((fine_cols, LANES), lambda s: (0, 0)),
        ],
        out_specs=pl.BlockSpec((levels, packed, rows, LANES), lambda s: (s, 0, 0, 0)),
        out_shape=jax.ShapeDtypeStruct((wide_count * levels, packed, rows, LANES), jnp.float32),
        scratch_shapes=[pltpu.VMEM((levels * fine_rows, LANES), jnp.float32)],
        name="pack",
    )(trajectory, innovation, background, obs_weight, pool)
    sent = sent.reshape(wide_count, levels * packed, rows, LANES)

    place = jnp.arange(padded, dtype=jnp.int32)
    row_index = jnp.where(place < rows + HALO, place, place - padded) + narrow_index * rows
    wavenumber = jnp.arange(cycle, dtype=jnp.int32)
    folded = jnp.minimum(wavenumber, cycle - wavenumber).astype(jnp.float32)
    latitude = jnp.pi * ((row_index.astype(jnp.float32) + 0.5) / total_rows - 0.5)
    cutoff = 0.5 * cycle * jnp.cos(latitude)
    inside = (row_index >= 0) & (row_index < total_rows)
    cutoff = jnp.where(inside, cutoff, 1.0)
    response = 1.0 / (1.0 + (folded[None, :] / cutoff[:, None]) ** 4)
    response = jnp.where(inside[:, None], response, 0.0) / cycle

    phase = np.arange(cycle)[:, None] * np.arange(cycle)[None, :] % cycle
    wave = np.cos(2.0 * np.pi / cycle * phase) + np.sin(2.0 * np.pi / cycle * phase)
    wave = wave.astype(np.float32)
    wave_high = wave.astype(jnp.bfloat16)
    wave_low = (wave - wave_high.astype(np.float32)).astype(jnp.bfloat16)

    vmem = pl.BlockSpec(memory_space=pltpu.VMEM)
    anywhere = pl.BlockSpec(memory_space=pl.ANY)
    f32 = jnp.float32
    moved_back = pl.pallas_call(
        functools.partial(sweep_kernel, wide_count, narrow_count, levels, chunk),
        in_specs=[anywhere, vmem, vmem, vmem],
        out_specs=anywhere,
        out_shape=jax.ShapeDtypeStruct((wide_count, groups, rows, LANES), f32),
        scratch_shapes=[
            pltpu.VMEM((wide_count, levels * packed, rows, LANES), f32),
            pltpu.VMEM((levels * ITEMS, padded, cycle), f32),
            pltpu.VMEM((groups * 4, rows, cycle), f32),
            pltpu.VMEM((wide_count, groups, rows, LANES), f32),
            pltpu.VMEM((levels * ITEMS, 8, cycle // 2), f32),
            pltpu.VMEM((levels * ITEMS, 8, cycle // 2), f32),
            pltpu.VMEM((levels * ITEMS, 8, cycle // 2), f32),
            pltpu.VMEM((levels * ITEMS, 8, cycle // 2), f32),
            pltpu.SemaphoreType.DMA((2,)),
            pltpu.SemaphoreType.DMA((wide_count,)),
            pltpu.SemaphoreType.DMA((wide_count,)),
            pltpu.SemaphoreType.DMA((2,)),
            pltpu.SemaphoreType.DMA((2,)),
            pltpu.SemaphoreType.DMA((wide_count,)),
            pltpu.SemaphoreType.DMA((wide_count,)),
        ],
        compiler_params=pltpu.CompilerParams(collective_id=0, has_side_effects=True),
        name="sweep",
    )(sent, response, jnp.asarray(wave_high), jnp.asarray(wave_low))

    return pl.pallas_call(
        finish_kernel,
        grid=(last + 1,),
        in_specs=[
            pl.BlockSpec((fields, levels, fine_rows, fine_cols), lambda s: (0, s, 0, 0)),
            pl.BlockSpec((1, groups, rows, LANES), lambda s: (s, 0, 0, 0)),
            pl.BlockSpec((LANES, 4 * LANES), lambda s: (0, 0)),
        ],
        out_specs=pl.BlockSpec((fields, levels, fine_rows, fine_cols), lambda s: (0, s, 0, 0)),
        out_shape=jax.ShapeDtypeStruct(trajectory.shape, jnp.bfloat16),
        scratch_shapes=[
            pltpu.VMEM((groups * rows, 4 * LANES), f32),
            pltpu.VMEM((fields * levels, fine_rows, fine_cols), f32),
        ],
        name="finish",
    )(trajectory, moved_back, spread)


def solution(mesh):
    in_specs = (
        P(None, None, "narrow", "wide"),
        P(None, None, "narrow", "wide"),
        P(None, None, "narrow", "wide"),
        P(None, "narrow", "wide"),
    )
    out_specs = P(None, None, "narrow", "wide")
    return jax.shard_map(shards, mesh=mesh, in_specs=in_specs, out_specs=out_specs, check_vma=False)
```

time: 197 us -> 81 us (0.41)
  Pallas kernels: 0 us -> 72.8 us
  waiting for transfers between devices: 67.1 us -> 0 us
  starting transfers between devices: 41.2 us -> 0 us
  local copies, waits for them, and re-layouts: 42.3 us -> 6.54 us
  blocking collectives: 21.9 us -> 0 us
  other arithmetic: 18.7 us -> 0.77 us
  matrix products: 4.62 us -> 0 us
    pallas_call x0 -> x3, Pallas kernels: none -> 72.8 us  [the longest x1 56.3 us: shards(): pl.pallas_call(functools.partial(sweep_kernel, wide_count, narrow_count,...]
    ppermute x16 -> x0, waiting for transfers between devices: 55 us -> none  [the longest x8 37.6 us: from_behind(): lax.ppermute(value, axis, [(source, source + steps) for source in range(f...]
    ppermute x16 -> x0, starting transfers between devices: 28.3 us -> none  [the longest x8 17.6 us: from_behind(): lax.ppermute(value, axis, [(source, source + steps) for source in range(f...]
    all_to_all x1 -> x0, blocking collectives: 21.9 us -> none  [shards(): lax.all_to_all(increment.reshape(FIELDS, LEVELS, 1, band_rows, cycle_size...]
    reshape x7 -> x0, local copies, waits for them, and re-layouts: 15.2 us -> none  [the longest x1 5.51 us: shards(): jnp.repeat(coarse_part, COARSEN, axis=3)]
    all_to_all x3 -> x0, starting transfers between devices: 12.9 us -> none  [the longest x1 5.2 us: shards(): lax.all_to_all(spread(background), 'wide', split_axis=2, concat_axis=4, t...]
    all_to_all x3 -> x0, waiting for transfers between devices: 12.1 us -> none  [the longest x1 10.8 us: shards(): lax.all_to_all(spread(background), 'wide', split_axis=2, concat_axis=4, t...]
    convert_element_type x2 -> x1, other arithmetic: 11.2 us -> 0.01 us  [shards(): folded = jnp.minimum(wavenumber, cycle - wavenumber).astype(jnp.float32)]
  transfers between devices with their start and end apart: 19 -> 0, of which waited for: 13 -> 0; matrix products, arithmetic and copies ran while one was open for 13% -> 0% of each run, Pallas kernels for 0% -> 0%
where the time goes in v1:
time: 81 us; the launch traced here: 80.1 us
  Pallas kernels  72.8 us (90%)
  local copies, waits for them, and re-layouts  6.54 us (8%)
    pallas_call x1, Pallas kernels, shards(): pl.pallas_call(functools.partial(sweep_kernel, wide_count, narrow_count,...  56.3 us
    pallas_call x1, Pallas kernels, shards(): pl.pallas_call(finish_kernel, grid=(last + 1,), in_specs=[pl.BlockSpec((f...  8.93 us
    pallas_call x1, Pallas kernels, shards(): pl.pallas_call(pack_kernel, grid=(wide_count,), in_specs=[pl.BlockSpec((1...  7.61 us
    unnamed x7, local copies, waits for them, and re-layouts  6.54 us

profile of v1, /device:TPU:0, one launch (start us, length us, event | category | flops | bytes accessed | tf_op | source)
XLA Modules:
  0.0 80.1 jit_solution(12161461784108413175)
XLA Ops:
  0.0 0.0 copy-start
  0.0 3.3 %copy.9.depart_ref = f32[5,72,16,32]{3,2,1,0:T(8,128)} copy(f32[5,72,16,32]{1,3,2,0:T(8,128)} %param.9) | data formatting | bytes 1474560 | tf_op args[1]
  3.3 0.0 copy-done
  3.3 0.0 copy-start.1
  3.3 2.2 %copy.10.back_ref = f32[5,72,16,32]{3,2,1,0:T(8,128)} copy(f32[5,72,16,32]{1,3,2,0:T(8,128)S(1)} %copy-done) | data formatting | bytes 1474560 | tf_op args[2]
  5.5 0.0 copy-done.1
  5.5 1.1 %copy.11.weight_ref = f32[72,16,32]{2,1,0:T(8,128)} copy(f32[72,16,32]{0,2,1:T(8,128)S(1)} %copy-done.1) | data formatting | bytes 294912 | tf_op args[3]
  6.5 7.6 %pack.1 = f32[72,3,16,128]{3,2,1,0:T(8,128)} custom-call(bf16[5,72,64,128]{3,2,1,0:T(8,128)(2,1)} %traj_ref.3, f32[5,72,16,32]{3,2,1,0:T(8,128)} %copy.9.depart_ref, f32[5,72,16,32]{3,2,1,0:T(8,128)} %copy.10.back_ref, f32[72,16,32]{2,1,0:T(8,128)} %copy.11.weight_ref, bf16[128,128]{1,0:T(8,128)(2,1)} %constant.44.clone.pool_ref), custom_call_target="tpu_custom_call" | custom-call | tf_op jit(solution)/shard_map/pack/pallas_call | solution.py:310
  14.1 0.1 multiply_select_fusion
  14.2 0.7 fusion.4.response_ref
  14.9 56.3 %sweep.1.inc_ref = f32[8,12,16,128]{3,2,1,0:T(8,128)} custom-call(f32[8,27,16,128]{3,2,1,0:T(8,128)} %bitcast.1, f32[24,256]{1,0:T(8,128)} %fusion.4.response_ref, bf16[256,256]{1,0:T(8,128)(2,1)} %constant.46.clone.wave_high_ref, bf16[256,256]{1,0:T(8,128)(2,1)} %constant.47.clone.wave_low_ref), custom_call_target="tpu_custom_call" | custom-call | tf_op jit(solution)/shard_map/sweep/pallas_call | solution.py:347
  71.2 8.9 %finish.1 = bf16[5,72,64,128]{3,2,1,0:T(8,128)(2,1)} custom-call(bf16[5,72,64,128]{3,2,1,0:T(8,128)(2,1)} %traj_ref.3, f32[8,12,16,128]{3,2,1,0:T(8,128)} %sweep.1.inc_ref, bf16[128,512]{1,0:T(8,128)(2,1)} %constant.45.clone.spread_ref), custom_call_target="tpu_custom_call" | custom-call | tf_op jit(solution)/shard_map/finish/pallas_call | solution.py:373
  (2 shorter events, 0.0 us)
Async XLA Ops:
  0.0 3.3 %copy-start = (f32[5,72,16,32]{1,3,2,0:T(8,128)S(1)}, f32[5,72,16,32]{1,3,2,0:T(8,128)}, u32[]{:S(2)}) copy-start(f32[5,72,16,32]{1,3,2,0:T(8,128)} %param.10) | copy-start | bytes 2211844
  3.3 2.2 %copy-start.1 = (f32[72,16,32]{0,2,1:T(8,128)S(1)}, f32[72,16,32]{0,2,1:T(8,128)}, u32[]{:S(2)}) copy-start(f32[72,16,32]{0,2,1:T(8,128)} %param.11) | copy-start | bytes 442372

commit v2 on v1

--- a/solution.py
+++ b/solution.py
@@ -122,22 +122,22 @@
     neighbours = has_above.astype(jnp.int32) + has_below.astype(jnp.int32)
     pl.semaphore_wait(barrier, wide_count - 1 + neighbours)
 
-    sends = []
-    for k in range(1, wide_count):
-        peer = lax.rem(me + k, wide_count)
-        copy = pltpu.make_async_remote_copy(
-            src_ref=x_ref.at[peer],
-            dst_ref=landed.at[me],
-            send_sem=send_sem.at[k],
-            recv_sem=recv_sem.at[k],
-            device_id=(peer, band),
-            device_id_type=MESH,
-        )
-        copy.start()
-        sends.append(copy)
-    keep.wait()
-    for copy in sends:
-        copy.wait_recv()
+    turns = levels // chunk
+    packed = chunk * (ITEMS // 4)
+    sends = [[None] * wide_count for _ in range(turns)]
+    for turn in range(turns):
+        for k in range(1, wide_count):
+            peer = lax.rem(me + k, wide_count)
+            copy = pltpu.make_async_remote_copy(
+                src_ref=x_ref.at[peer, pl.ds(turn * packed, packed)],
+                dst_ref=landed.at[me, pl.ds(turn * packed, packed)],
+                send_sem=send_sem.at[turn, k],
+                recv_sem=recv_sem.at[turn, k],
+                device_id=(peer, band),
+                device_id_type=MESH,
+            )
+            copy.start()
+            sends[turn][k] = copy
 
     low_half = lax.broadcasted_iota(jnp.int32, (8, half), 0) < HALO
 
@@ -155,24 +155,19 @@
             down_out[at] = jnp.where(low_half, pltpu.roll(bottom[:, :half], HALO, 0), bottom[:, half:])
         return carry
 
-    lax.fori_loop(0, levels, unpack, 0)
-
-    up_copy = pltpu.make_async_remote_copy(
-        src_ref=up_out, dst_ref=up_in, send_sem=halo_send.at[0], recv_sem=halo_recv.at[0],
-        device_id=(me, band - 1), device_id_type=MESH,
-    )
-    down_copy = pltpu.make_async_remote_copy(
-        src_ref=down_out, dst_ref=down_in, send_sem=halo_send.at[1], recv_sem=halo_recv.at[1],
-        device_id=(me, band + 1), device_id_type=MESH,
-    )
-
-    @pl.when(has_above)
-    def _():
-        up_copy.start()
-
-    @pl.when(has_below)
-    def _():
-        down_copy.start()
+    def halo_copies(turn):
+        part = pl.ds(turn * chunk * ITEMS, chunk * ITEMS)
+        up_copy = pltpu.make_async_remote_copy(
+            src_ref=up_out.at[part], dst_ref=up_in.at[part],
+            send_sem=halo_send.at[turn, 0], recv_sem=halo_recv.at[turn, 0],
+            device_id=(me, band - 1), device_id_type=MESH,
+        )
+        down_copy = pltpu.make_async_remote_copy(
+            src_ref=down_out.at[part], dst_ref=down_in.at[part],
+            send_sem=halo_send.at[turn, 1], recv_sem=halo_recv.at[turn, 1],
+            device_id=(me, band + 1), device_id_type=MESH,
+        )
+        return up_copy, down_copy
 
     @pl.when(jnp.logical_not(has_below))
     def _():
@@ -181,14 +176,6 @@
     @pl.when(jnp.logical_not(has_above))
     def _():
         down_in[...] = jnp.zeros_like(down_in)
-
-    @pl.when(has_below)
-    def _():
-        up_copy.wait_recv()
-
-    @pl.when(has_above)
-    def _():
-        down_copy.wait_recv()
 
     def take_halo(level, carry):
         for item in range(ITEMS):
@@ -197,8 +184,6 @@
             fields[at, rows:padded, 0:half] = jnp.where(low_half, below, pltpu.roll(above, HALO, 0))
             fields[at, rows:padded, half:cycle] = jnp.where(low_half, pltpu.roll(below, HALO, 0), above)
         return carry
-
-    lax.fori_loop(0, levels, take_halo, 0)
 
     def zonal(q):
         shape = q.shape
@@ -209,7 +194,7 @@
         high, low = split_bf16(spectrum.reshape(-1, cycle))
         return (dot(high, wave_high) + dot(low, wave_high) + dot(high, wave_low)).reshape(shape)
 
-    def sweep(turn, carry):
+    def sweep(turn):
         at = turn * chunk
         block = fields[pl.ds(at * ITEMS, chunk * ITEMS)].reshape(chunk, ITEMS, padded, cycle)
         background = block[:, :FIELDS]
@@ -223,52 +208,92 @@
         for _ in range(STEPS):
             costate = stencil_transposed(zonal(costate), drift)
         increment = background - descent_step * ((background - background) + costate)
-        result[pl.ds(at * FIELDS, chunk * FIELDS)] = increment.reshape(chunk * FIELDS, padded, cycle)[:, :rows]
-        return carry
-
-    lax.fori_loop(0, levels // chunk, sweep, 0)
-
-    def repack(group, carry):
-        for tile in range(cycle // LANES):
-            parts = [result[4 * group + j, :, tile * LANES : (tile + 1) * LANES] for j in range(4)]
-            for m, value in enumerate(block_transpose(parts, cols)):
-                outgoing[4 * tile + m, group] = value
-        return carry
-
-    lax.fori_loop(0, groups, repack, 0)
-
-    keep_back = pltpu.make_async_copy(outgoing.at[me], out_ref.at[me], local_sem.at[1])
-    keep_back.start()
+        result[0 : chunk * FIELDS] = increment.reshape(chunk * FIELDS, padded, cycle)[:, :rows]
+
+    each = groups // turns
+
+    def send_back(turn):
+        def repack(group, carry):
+            for tile in range(cycle // LANES):
+                parts = [result[4 * group + j, :, tile * LANES : (tile + 1) * LANES] for j in range(4)]
+                for m, value in enumerate(block_transpose(parts, cols)):
+                    outgoing[4 * tile + m, turn * each + group] = value
+            return carry
+
+        lax.fori_loop(0, each, repack, 0)
+        part = pl.ds(turn * each, each)
+        keep_back = pltpu.make_async_copy(
+            outgoing.at[me, part], out_ref.at[me, part], back_send.at[turn, 0]
+        )
+        keep_back.start()
+        backs = [keep_back]
+        for k in range(1, wide_count):
+            peer = lax.rem(me + k, wide_count)
+            copy = pltpu.make_async_remote_copy(
+                src_ref=outgoing.at[peer, part],
+                dst_ref=out_ref.at[me, part],
+                send_sem=back_send.at[turn, k],
+                recv_sem=back_recv.at[turn, k],
+                device_id=(peer, band),
+                device_id_type=MESH,
+            )
+            copy.start()
+            backs.append(copy)
+        return backs
+
+    def compute(turn):
+        up_copy, down_copy = halo_copies(turn)
+
+        @pl.when(has_below)
+        def _():
+            up_copy.wait_recv()
+
+        @pl.when(has_above)
+        def _():
+            down_copy.wait_recv()
+
+        lax.fori_loop(turn * chunk, (turn + 1) * chunk, take_halo, 0)
+        sweep(turn)
+        return send_back(turn)
+
+    keep.wait()
     backs = []
-    for k in range(1, wide_count):
-        peer = lax.rem(me + k, wide_count)
-        copy = pltpu.make_async_remote_copy(
-            src_ref=outgoing.at[peer],
-            dst_ref=out_ref.at[me],
-            send_sem=back_send.at[k],
-            recv_sem=back_recv.at[k],
-            device_id=(peer, band),
-            device_id_type=MESH,
-        )
-        copy.start()
-        backs.append(copy)
-    for copy in sends:
-        copy.wait_send()
-
-    @pl.when(has_above)
-    def _():
-        up_copy.wait_send()
-
-    @pl.when(has_below)
-    def _():
-        down_copy.wait_send()
-
-    keep_back.wait()
+    for turn in range(turns):
+        for k in range(1, wide_count):
+            sends[turn][k].wait_recv()
+        lax.fori_loop(turn * chunk, (turn + 1) * chunk, unpack, 0)
+        up_copy, down_copy = halo_copies(turn)
+
+        @pl.when(has_above)
+        def _():
+            up_copy.start()
+
+        @pl.when(has_below)
+        def _():
+            down_copy.start()
+
+        if turn > 0:
+            backs += compute(turn - 1)
+    backs += compute(turns - 1)
+
+    for turn in range(turns):
+        for k in range(1, wide_count):
+            sends[turn][k].wait_send()
+        up_copy, down_copy = halo_copies(turn)
+
+        @pl.when(has_above)
+        def _():
+            up_copy.wait_send()
+
+        @pl.when(has_below)
+        def _():
+            down_copy.wait_send()
+
     for copy in backs:
         copy.wait()
 
 
-def finish_kernel(traj_ref, inc_ref, spread_ref, out_ref, wide, tall):
+def finish_kernel(chunk, traj_ref, inc_ref, spread_ref, out_ref, wide, tall):
     fields, levels, fine_rows, fine_cols = traj_ref.shape
     groups, rows = inc_ref.shape[1:3]
     high, low = split_bf16(inc_ref[0].reshape(groups * rows, LANES))
@@ -276,7 +301,8 @@
     for level in range(levels):
         for f in range(fields):
             item = level * fields + f
-            group, j = divmod(item, 4)
+            turn, place = divmod(item, chunk * fields)
+            group, j = turn * (groups // (levels // chunk)) + place // 4, place % 4
             part = wide[group * rows : (group + 1) * rows, j * LANES : (j + 1) * LANES]
             for t in range(COARSEN):
                 tall[item, pl.ds(t, rows, stride=COARSEN), :] = part
@@ -295,7 +321,8 @@
     last = -(-total_levels // levels) - 1
     chunk = max(c for c in range(1, 6) if levels % c == 0)
     packed = ITEMS // 4
-    groups = -(-fields * levels // 4)
+    turns = levels // chunk
+    groups = turns * -(-fields * chunk // 4)
     padded = rows + 2 * HALO
 
     lane = np.arange(fine_cols)
@@ -352,26 +379,26 @@
         scratch_shapes=[
             pltpu.VMEM((wide_count, levels * packed, rows, LANES), f32),
             pltpu.VMEM((levels * ITEMS, padded, cycle), f32),
-            pltpu.VMEM((groups * 4, rows, cycle), f32),
+            pltpu.VMEM((groups // turns * 4, rows, cycle), f32),
             pltpu.VMEM((wide_count, groups, rows, LANES), f32),
             pltpu.VMEM((levels * ITEMS, 8, cycle // 2), f32),
             pltpu.VMEM((levels * ITEMS, 8, cycle // 2), f32),
             pltpu.VMEM((levels * ITEMS, 8, cycle // 2), f32),
             pltpu.VMEM((levels * ITEMS, 8, cycle // 2), f32),
-            pltpu.SemaphoreType.DMA((2,)),
-            pltpu.SemaphoreType.DMA((wide_count,)),
-            pltpu.SemaphoreType.DMA((wide_count,)),
-            pltpu.SemaphoreType.DMA((2,)),
-            pltpu.SemaphoreType.DMA((2,)),
-            pltpu.SemaphoreType.DMA((wide_count,)),
-            pltpu.SemaphoreType.DMA((wide_count,)),
+            pltpu.SemaphoreType.DMA((1,)),
+            pltpu.SemaphoreType.DMA((turns, wide_count)),
+            pltpu.SemaphoreType.DMA((turns, wide_count)),
+            pltpu.SemaphoreType.DMA((turns, 2)),
+            pltpu.SemaphoreType.DMA((turns, 2)),
+            pltpu.SemaphoreType.DMA((turns, wide_count)),
+            pltpu.SemaphoreType.DMA((turns, wide_count)),
         ],
         compiler_params=pltpu.CompilerParams(collective_id=0, has_side_effects=True),
         name="sweep",
     )(sent, response, jnp.asarray(wave_high), jnp.asarray(wave_low))
 
     return pl.pallas_call(
-        finish_kernel,
+        functools.partial(finish_kernel, chunk),
         grid=(last + 1,),
         in_specs=[
             pl.BlockSpec((fields, levels, fine_rows, fine_cols), lambda s: (0, s, 0, 0)),

time: 81 us -> 66.1 us (0.82)
  Pallas kernels: 72.8 us -> 58.3 us
    pallas_call x1, Pallas kernels: 56.3 us -> 41.8 us  [shards(): pl.pallas_call(functools.partial(sweep_kernel, wide_count, narrow_count,...]
where the time goes in v2:
time: 66.1 us; the launch traced here: 65.6 us
  Pallas kernels  58.3 us (88%)
  local copies, waits for them, and re-layouts  6.54 us (10%)
  other arithmetic  0.77 us (1%)
    pallas_call x1, Pallas kernels, shards(): pl.pallas_call(functools.partial(sweep_kernel, wide_count, narrow_count,...  41.8 us
    pallas_call x1, Pallas kernels, shards(): pl.pallas_call(functools.partial(finish_kernel, chunk), grid=(last + 1,),...  8.91 us
    pallas_call x1, Pallas kernels, shards(): pl.pallas_call(pack_kernel, grid=(wide_count,), in_specs=[pl.BlockSpec((1...  7.61 us
    unnamed x7, local copies, waits for them, and re-layouts  6.54 us

profile of v2, /device:TPU:0, one launch (start us, length us, event | category | flops | bytes accessed | tf_op | source)
XLA Modules:
  0.0 65.6 jit_solution(13894486659070890929)
XLA Ops:
  0.0 0.0 copy-start
  0.0 3.3 %copy.9.depart_ref = f32[5,72,16,32]{3,2,1,0:T(8,128)} copy(f32[5,72,16,32]{1,3,2,0:T(8,128)} %param.9) | data formatting | bytes 1474560 | tf_op args[1]
  3.3 0.0 copy-done
  3.3 0.0 copy-start.1
  3.3 2.2 %copy.10.back_ref = f32[5,72,16,32]{3,2,1,0:T(8,128)} copy(f32[5,72,16,32]{1,3,2,0:T(8,128)S(1)} %copy-done) | data formatting | bytes 1474560 | tf_op args[2]
  5.5 0.0 copy-done.1
  5.5 1.1 %copy.11.weight_ref = f32[72,16,32]{2,1,0:T(8,128)} copy(f32[72,16,32]{0,2,1:T(8,128)S(1)} %copy-done.1) | data formatting | bytes 294912 | tf_op args[3]
  6.5 7.6 %pack.1 = f32[72,3,16,128]{3,2,1,0:T(8,128)} custom-call(bf16[5,72,64,128]{3,2,1,0:T(8,128)(2,1)} %traj_ref.3, f32[5,72,16,32]{3,2,1,0:T(8,128)} %copy.9.depart_ref, f32[5,72,16,32]{3,2,1,0:T(8,128)} %copy.10.back_ref, f32[72,16,32]{2,1,0:T(8,128)} %copy.11.weight_ref, bf16[128,128]{1,0:T(8,128)(2,1)} %constant.44.clone.pool_ref), custom_call_target="tpu_custom_call" | custom-call | tf_op jit(solution)/shard_map/pack/pallas_call | solution.py:337
  14.1 0.1 multiply_select_fusion
  14.2 0.7 %fusion.4.response_ref = f32[24,256]{1,0:T(8,128)} fusion(f32[24]{0:T(128)S(1)} %multiply_select_fusion, f32[256]{0:T(256)S(1)} %fusion.5, pred[24]{0:T(512)(128)(4,1)S(1)} %compare_and_fusion), kind=kLoop, calls=%fused_computation.5 | loop fusion | flops 43008 | bytes 25720 | tf_op jit(solution)/shard_map/div | solution.py:363
  14.9 41.8 %sweep.1.inc_ref = f32[8,12,16,128]{3,2,1,0:T(8,128)} custom-call(f32[8,27,16,128]{3,2,1,0:T(8,128)} %bitcast.1, f32[24,256]{1,0:T(8,128)} %fusion.4.response_ref, bf16[256,256]{1,0:T(8,128)(2,1)} %constant.46.clone.wave_high_ref, bf16[256,256]{1,0:T(8,128)(2,1)} %constant.47.clone.wave_low_ref), custom_call_target="tpu_custom_call" | custom-call | tf_op jit(solution)/shard_map/sweep/pallas_call | solution.py:374
  56.7 8.9 %finish.1 = bf16[5,72,64,128]{3,2,1,0:T(8,128)(2,1)} custom-call(bf16[5,72,64,128]{3,2,1,0:T(8,128)(2,1)} %traj_ref.3, f32[8,12,16,128]{3,2,1,0:T(8,128)} %sweep.1.inc_ref, bf16[128,512]{1,0:T(8,128)(2,1)} %constant.45.clone.spread_ref), custom_call_target="tpu_custom_call" | custom-call | tf_op jit(solution)/shard_map/finish/pallas_call | solution.py:400
  (2 shorter events, 0.0 us)
Async XLA Ops:
  0.0 3.3 %copy-start = (f32[5,72,16,32]{1,3,2,0:T(8,128)S(1)}, f32[5,72,16,32]{1,3,2,0:T(8,128)}, u32[]{:S(2)}) copy-start(f32[5,72,16,32]{1,3,2,0:T(8,128)} %param.10) | copy-start | bytes 2211844
  3.3 2.2 %copy-start.1 = (f32[72,16,32]{0,2,1:T(8,128)S(1)}, f32[72,16,32]{0,2,1:T(8,128)}, u32[]{:S(2)}) copy-start(f32[72,16,32]{0,2,1:T(8,128)} %param.11) | copy-start | bytes 442372

commit v3 on v2

--- a/solution.py
+++ b/solution.py
@@ -48,18 +48,31 @@
 
 def pack_kernel(traj_ref, depart_ref, back_ref, weight_ref, pool_ref, out_ref, sums):
     levels, fine_rows, fine_cols = traj_ref.shape[1:]
-    rows = fine_rows // COARSEN
-    cols = fine_cols // COARSEN
+    rows, cols = weight_ref.shape[:2]
     sums[...] = dot(traj_ref[0].reshape(levels * fine_rows, fine_cols), pool_ref[...])
     total = sums[pl.ds(0, levels * rows, stride=COARSEN), :]
     for t in range(1, COARSEN):
         total = total + sums[pl.ds(t, levels * rows, stride=COARSEN), :]
     drift = advection_scale * jnp.tanh(total * (1.0 / (COARSEN * COARSEN)))
-    drift = drift[:, :cols].reshape(levels, rows, cols)
-    items = [back_ref[f] for f in range(FIELDS)] + [drift, weight_ref[...]]
-    items += [depart_ref[f] for f in range(FIELDS)]
+    drift = drift.reshape(levels, rows, LANES)
+    is_drift = lax.broadcasted_iota(jnp.int32, drift.shape, 2) // cols == 1
+
+    def item(index, row):
+        if index < FIELDS:
+            return back_ref[index, row]
+        if index < FIELDS + 2:
+            return weight_ref[row]
+        return depart_ref[index - FIELDS - 2, row]
+
     for group in range(ITEMS // 4):
-        out_ref[:, group] = jnp.concatenate(items[4 * group : 4 * group + 4], axis=-1)
+        lines = []
+        for row in range(rows):
+            stacked = jnp.concatenate([item(4 * group + j, row) for j in range(4)], axis=0)
+            lines.append(stacked.T)
+        value = jnp.swapaxes(jnp.stack(lines), 0, 1)
+        if group == FIELDS // 4:
+            value = jnp.where(is_drift, drift, value)
+        out_ref[:, group] = value
 
 
 def stencil(q, drift):
@@ -327,7 +340,7 @@
 
     lane = np.arange(fine_cols)
     pool = np.zeros((fine_cols, LANES), np.float32)
-    pool[lane, lane // COARSEN] = 1.0
+    pool[lane, FIELDS % 4 * cols + lane // COARSEN] = 1.0
     spread = np.zeros((LANES, 4 * LANES), np.float32)
     for j in range(4):
         spread[j * cols + lane // COARSEN, j * LANES + lane] = 1.0
@@ -336,19 +349,25 @@
 
     sent = pl.pallas_call(
         pack_kernel,
-        grid=(wide_count,),
+        grid=(rows // 8,),
         in_specs=[
-            pl.BlockSpec((1, levels, fine_rows, fine_cols), lambda s: (0, jnp.minimum(s, last), 0, 0)),
-            pl.BlockSpec((fields, levels, rows, cols), lambda s: (0, jnp.minimum(s, last), 0, 0)),
-            pl.BlockSpec((fields, levels, rows, cols), lambda s: (0, jnp.minimum(s, last), 0, 0)),
-            pl.BlockSpec((levels, rows, cols), lambda s: (jnp.minimum(s, last), 0, 0)),
-            pl.BlockSpec((fine_cols, LANES), lambda s: (0, 0)),
+            pl.BlockSpec((1, total_levels, 8 * COARSEN, fine_cols), lambda r: (0, 0, r, 0)),
+            pl.BlockSpec((fields, 8, cols, total_levels), lambda r: (0, r, 0, 0)),
+            pl.BlockSpec((fields, 8, cols, total_levels), lambda r: (0, r, 0, 0)),
+            pl.BlockSpec((8, cols, total_levels), lambda r: (r, 0, 0)),
+            pl.BlockSpec((fine_cols, LANES), lambda r: (0, 0)),
         ],
-        out_specs=pl.BlockSpec((levels, packed, rows, LANES), lambda s: (s, 0, 0, 0)),
+        out_specs=pl.BlockSpec((total_levels, packed, 8, LANES), lambda r: (0, 0, r, 0)),
         out_shape=jax.ShapeDtypeStruct((wide_count * levels, packed, rows, LANES), jnp.float32),
-        scratch_shapes=[pltpu.VMEM((levels * fine_rows, LANES), jnp.float32)],
+        scratch_shapes=[pltpu.VMEM((total_levels * 8 * COARSEN, LANES), jnp.float32)],
         name="pack",
-    )(trajectory, innovation, background, obs_weight, pool)
+    )(
+        trajectory,
+        innovation.transpose(0, 2, 3, 1),
+        background.transpose(0, 2, 3, 1),
+        obs_weight.transpose(1, 2, 0),
+        pool,
+    )
     sent = sent.reshape(wide_count, levels * packed, rows, LANES)
 
     place = jnp.arange(padded, dtype=jnp.int32)

time: 66.1 us -> 55.3 us (0.84)
  local copies, waits for them, and re-layouts: 6.54 us -> 0 us
  Pallas kernels: 58.3 us -> 54.3 us
    unnamed x7 -> x0, local copies, waits for them, and re-layouts: 6.54 us -> none
    pallas_call x1, Pallas kernels: 7.61 us -> 3.58 us  [shards(): pl.pallas_call(pack_kernel, grid=(rows // 8,), in_specs=[pl.BlockSpec((1,...]
where the time goes in v3:
time: 55.3 us; the launch traced here: 55 us
  Pallas kernels  54.3 us (98%)
  other arithmetic  0.75 us (1%)
    pallas_call x1, Pallas kernels, shards(): pl.pallas_call(functools.partial(sweep_kernel, wide_count, narrow_count,...  41.8 us
    pallas_call x1, Pallas kernels, shards(): pl.pallas_call(functools.partial(finish_kernel, chunk), grid=(last + 1,),...  8.91 us
    pallas_call x1, Pallas kernels, shards(): pl.pallas_call(pack_kernel, grid=(rows // 8,), in_specs=[pl.BlockSpec((1,...  3.58 us

profile of v3, /device:TPU:0, one launch (start us, length us, event | category | flops | bytes accessed | tf_op | source)
XLA Modules:
  0.0 55.0 jit_solution(6080035976341146816)
XLA Ops:
  0.0 0.1 multiply_select_fusion
  0.1 0.7 %fusion.4.response_ref = f32[24,256]{1,0:T(8,128)} fusion(f32[24]{0:T(128)S(1)} %multiply_select_fusion, f32[256]{0:T(256)S(1)} %fusion.5, pred[24]{0:T(512)(128)(4,1)S(1)} %compare_and_fusion), kind=kLoop, calls=%fused_computation.5 | loop fusion | flops 43008 | bytes 25720 | tf_op jit(solution)/shard_map/div | solution.py:382
  0.8 3.6 %pack.1 = f32[72,3,16,128]{3,2,1,0:T(8,128)} custom-call(bf16[5,72,64,128]{3,2,1,0:T(8,128)(2,1)} %traj_ref.3, f32[5,16,32,72]{3,2,1,0:T(8,128)} %bitcast.5, f32[5,16,32,72]{3,2,1,0:T(8,128)} %bitcast.6, f32[16,32,72]{2,1,0:T(8,128)} %bitcast.7, bf16[128,128]{1,0:T(8,128)(2,1)} %constant.44.clone.pool_ref), custom_call_target="tpu_custom_call" | custom-call | tf_op jit(solution)/shard_map/pack/pallas_call | solution.py:350
  4.3 41.8 %sweep.1.inc_ref = f32[8,12,16,128]{3,2,1,0:T(8,128)} custom-call(f32[8,27,16,128]{3,2,1,0:T(8,128)} %bitcast.4, f32[24,256]{1,0:T(8,128)} %fusion.4.response_ref, bf16[256,256]{1,0:T(8,128)(2,1)} %constant.46.clone.wave_high_ref, bf16[256,256]{1,0:T(8,128)(2,1)} %constant.47.clone.wave_low_ref), custom_call_target="tpu_custom_call" | custom-call | tf_op jit(solution)/shard_map/sweep/pallas_call | solution.py:393
  46.1 8.9 %finish.1 = bf16[5,72,64,128]{3,2,1,0:T(8,128)(2,1)} custom-call(bf16[5,72,64,128]{3,2,1,0:T(8,128)(2,1)} %traj_ref.3, f32[8,12,16,128]{3,2,1,0:T(8,128)} %sweep.1.inc_ref, bf16[128,512]{1,0:T(8,128)(2,1)} %constant.45.clone.spread_ref), custom_call_target="tpu_custom_call" | custom-call | tf_op jit(solution)/shard_map/finish/pallas_call | solution.py:419
  (2 shorter events, 0.0 us)

commit v4 on v3

--- a/solution.py
+++ b/solution.py
@@ -306,20 +306,22 @@
         copy.wait()
 
 
-def finish_kernel(chunk, traj_ref, inc_ref, spread_ref, out_ref, wide, tall):
+def finish_kernel(chunk, traj_ref, inc_ref, spread_ref, out_ref, tall):
     fields, levels, fine_rows, fine_cols = traj_ref.shape
     groups, rows = inc_ref.shape[1:3]
-    high, low = split_bf16(inc_ref[0].reshape(groups * rows, LANES))
-    wide[...] = dot(high, spread_ref[...]) + dot(low, spread_ref[...])
-    for level in range(levels):
-        for f in range(fields):
-            item = level * fields + f
-            turn, place = divmod(item, chunk * fields)
-            group, j = turn * (groups // (levels // chunk)) + place // 4, place % 4
-            part = wide[group * rows : (group + 1) * rows, j * LANES : (j + 1) * LANES]
-            for t in range(COARSEN):
-                tall[item, pl.ds(t, rows, stride=COARSEN), :] = part
-            out_ref[f, level] = (traj_ref[f, level].astype(jnp.float32) + tall[item]).astype(jnp.bfloat16)
+    part = inc_ref[0].reshape(groups * rows, LANES)
+    for t in range(COARSEN):
+        tall[pl.ds(t, groups * rows, stride=COARSEN), :] = part
+    each = groups // (levels // chunk)
+    for turn in range(levels // chunk):
+        span = each * fine_rows
+        operand = jnp.concatenate(split_bf16(tall[turn * span : (turn + 1) * span]), axis=1)
+        wide = dot(operand, spread_ref[...])
+        for place in range(chunk * fields):
+            level, f = divmod(turn * chunk * fields + place, fields)
+            group, j = divmod(place, 4)
+            fine = wide[group * fine_rows : (group + 1) * fine_rows, j * LANES : (j + 1) * LANES]
+            out_ref[f, level] = (traj_ref[f, level].astype(jnp.float32) + fine).astype(jnp.bfloat16)
 
 
 def shards(trajectory, innovation, background, obs_weight):
@@ -345,7 +347,7 @@
     for j in range(4):
         spread[j * cols + lane // COARSEN, j * LANES + lane] = 1.0
     pool = jnp.asarray(pool, jnp.bfloat16)
-    spread = jnp.asarray(spread, jnp.bfloat16)
+    spread = jnp.asarray(np.concatenate([spread, spread]), jnp.bfloat16)
 
     sent = pl.pallas_call(
         pack_kernel,
@@ -422,13 +424,12 @@
         in_specs=[
             pl.BlockSpec((fields, levels, fine_rows, fine_cols), lambda s: (0, s, 0, 0)),
             pl.BlockSpec((1, groups, rows, LANES), lambda s: (s, 0, 0, 0)),
-            pl.BlockSpec((LANES, 4 * LANES), lambda s: (0, 0)),
+            pl.BlockSpec((2 * LANES, 4 * LANES), lambda s: (0, 0)),
         ],
         out_specs=pl.BlockSpec((fields, levels, fine_rows, fine_cols), lambda s: (0, s, 0, 0)),
         out_shape=jax.ShapeDtypeStruct(trajectory.shape, jnp.bfloat16),
         scratch_shapes=[
-            pltpu.VMEM((groups * rows, 4 * LANES), f32),
-            pltpu.VMEM((fields * levels, fine_rows, fine_cols), f32),
+            pltpu.VMEM((groups * fine_rows, LANES), f32),
         ],
         name="finish",
     )(trajectory, moved_back, spread)

time: 55.3 us -> 55.5 us (level)
  no operation moved by 1% of the time
where the time goes in v4:
time: 55.5 us; the launch traced here: 55.1 us
  Pallas kernels  54.4 us (98%)
  other arithmetic  0.75 us (1%)
    pallas_call x1, Pallas kernels, shards(): pl.pallas_call(functools.partial(sweep_kernel, wide_count, narrow_count,...  41.8 us
    pallas_call x1, Pallas kernels, shards(): pl.pallas_call(functools.partial(finish_kernel, chunk), grid=(last + 1,),...  9.02 us
    pallas_call x1, Pallas kernels, shards(): pl.pallas_call(pack_kernel, grid=(rows // 8,), in_specs=[pl.BlockSpec((1,...  3.58 us

profile of v4, /device:TPU:0, one launch (start us, length us, event | category | flops | bytes accessed | tf_op | source)
XLA Modules:
  0.0 55.1 jit_solution(8449399268457844768)
XLA Ops:
  0.0 0.1 multiply_select_fusion
  0.1 0.7 %fusion.4.response_ref = f32[24,256]{1,0:T(8,128)} fusion(f32[24]{0:T(128)S(1)} %multiply_select_fusion, f32[256]{0:T(256)S(1)} %fusion.5, pred[24]{0:T(512)(128)(4,1)S(1)} %compare_and_fusion), kind=kLoop, calls=%fused_computation.5 | loop fusion | flops 43008 | bytes 25720 | tf_op jit(solution)/shard_map/div | solution.py:384
  0.8 3.6 %pack.1 = f32[72,3,16,128]{3,2,1,0:T(8,128)} custom-call(bf16[5,72,64,128]{3,2,1,0:T(8,128)(2,1)} %traj_ref.3, f32[5,16,32,72]{3,2,1,0:T(8,128)} %bitcast.5, f32[5,16,32,72]{3,2,1,0:T(8,128)} %bitcast.6, f32[16,32,72]{2,1,0:T(8,128)} %bitcast.7, bf16[128,128]{1,0:T(8,128)(2,1)} %constant.44.clone.pool_ref), custom_call_target="tpu_custom_call" | custom-call | tf_op jit(solution)/shard_map/pack/pallas_call | solution.py:352
  4.3 41.8 %sweep.1.inc_ref = f32[8,12,16,128]{3,2,1,0:T(8,128)} custom-call(f32[8,27,16,128]{3,2,1,0:T(8,128)} %bitcast.4, f32[24,256]{1,0:T(8,128)} %fusion.4.response_ref, bf16[256,256]{1,0:T(8,128)(2,1)} %constant.46.clone.wave_high_ref, bf16[256,256]{1,0:T(8,128)(2,1)} %constant.47.clone.wave_low_ref), custom_call_target="tpu_custom_call" | custom-call | tf_op jit(solution)/shard_map/sweep/pallas_call | solution.py:395
  46.1 9.0 %finish.1 = bf16[5,72,64,128]{3,2,1,0:T(8,128)(2,1)} custom-call(bf16[5,72,64,128]{3,2,1,0:T(8,128)(2,1)} %traj_ref.3, f32[8,12,16,128]{3,2,1,0:T(8,128)} %sweep.1.inc_ref, bf16[256,512]{1,0:T(8,128)(2,1)} %constant.45.clone.spread_ref), custom_call_target="tpu_custom_call" | custom-call | tf_op jit(solution)/shard_map/finish/pallas_call | solution.py:421
  (2 shorter events, 0.0 us)

commit v5 on v4

--- a/solution.py
+++ b/solution.py
@@ -414,7 +414,9 @@
             pltpu.SemaphoreType.DMA((turns, wide_count)),
             pltpu.SemaphoreType.DMA((turns, wide_count)),
         ],
-        compiler_params=pltpu.CompilerParams(collective_id=0, has_side_effects=True),
+        compiler_params=pltpu.CompilerParams(
+            collective_id=0, has_side_effects=True, vmem_limit_bytes=32 * 1024 * 1024
+        ),
         name="sweep",
     )(sent, response, jnp.asarray(wave_high), jnp.asarray(wave_low))
 
@@ -431,6 +433,7 @@
         scratch_shapes=[
             pltpu.VMEM((groups * fine_rows, LANES), f32),
         ],
+        compiler_params=pltpu.CompilerParams(vmem_limit_bytes=32 * 1024 * 1024),
         name="finish",
     )(trajectory, moved_back, spread)
 

time: 55.5 us -> 54.4 us (0.980)
  Pallas kernels: 54.4 us -> 49.9 us
  local copies, waits for them, and re-layouts: 0 us -> 4.16 us
  other arithmetic: 0.75 us -> 0.15 us
    unnamed x0 -> x10, local copies, waits for them, and re-layouts: none -> 4.16 us
    pallas_call x1, Pallas kernels: 9.02 us -> 5.66 us  [shards(): pl.pallas_call(functools.partial(finish_kernel, chunk), grid=(last + 1,),...]
    pallas_call x1, Pallas kernels: 41.8 us -> 40.5 us  [shards(): pl.pallas_call(functools.partial(sweep_kernel, wide_count, narrow_count,...]
    div x1, other arithmetic: 0.69 us -> 0.09 us  [shards(): response = jnp.where(inside[:, None], response, 0.0) / cycle]
where the time goes in v5:
time: 54.4 us; the launch traced here: 54.2 us
  Pallas kernels  49.9 us (92%)
  local copies, waits for them, and re-layouts  4.16 us (8%)
    pallas_call x1, Pallas kernels, shards(): pl.pallas_call(functools.partial(sweep_kernel, wide_count, narrow_count,...  40.5 us
    pallas_call x1, Pallas kernels, shards(): pl.pallas_call(functools.partial(finish_kernel, chunk), grid=(last + 1,),...  5.66 us
    unnamed x10, local copies, waits for them, and re-layouts  4.16 us
    pallas_call x1, Pallas kernels, shards(): pl.pallas_call(pack_kernel, grid=(rows // 8,), in_specs=[pl.BlockSpec((1,...  3.68 us

profile of v5, /device:TPU:0, one launch (start us, length us, event | category | flops | bytes accessed | tf_op | source)
XLA Modules:
  0.0 54.2 jit_solution(2871133146162457420)
XLA Ops:
  0.0 0.1 multiply_select_fusion
  0.1 0.1 fusion.4.response_ref
  0.2 0.0 copy-start.3
  0.2 0.0 copy-start.4
  0.2 3.7 %pack.1 = f32[72,3,16,128]{3,2,1,0:T(8,128)} custom-call(bf16[5,72,64,128]{3,2,1,0:T(8,128)(2,1)} %traj_ref.3, f32[5,16,32,72]{3,2,1,0:T(8,128)} %bitcast.5, f32[5,16,32,72]{3,2,1,0:T(8,128)} %bitcast.6, f32[16,32,72]{2,1,0:T(8,128)} %bitcast.7, bf16[128,128]{1,0:T(8,128)(2,1)} %constant.44.clone.pool_ref), custom_call_target="tpu_custom_call" | custom-call | tf_op jit(solution)/shard_map/pack/pallas_call | solution.py:352
  3.9 0.0 copy-done.3
  3.9 0.0 copy-done.4
  3.9 0.0 copy-start.1
  3.9 1.5 %copy-done.1 = f32[72,3,16,128]{3,2,1,0:T(8,128)S(1)} copy-done((f32[72,3,16,128]{3,2,1,0:T(8,128)S(1)}, f32[72,3,16,128]{3,2,1,0:T(8,128)}, u32[]{:S(2)}) %copy-start.1) | copy-done | bytes 1769496
  5.4 0.0 copy-start.2
  5.4 40.5 %sweep.1.inc_ref = f32[8,12,16,128]{3,2,1,0:T(8,128)S(1)} custom-call(f32[8,27,16,128]{3,2,1,0:T(8,128)S(1)} %bitcast.4, f32[24,256]{1,0:T(8,128)S(1)} %fusion.4.response_ref, bf16[256,256]{1,0:T(8,128)(2,1)S(1)} %copy-done.4, bf16[256,256]{1,0:T(8,128)(2,1)S(1)} %copy-done.3), custom_call_target="tpu_custom_call" | custom-call | tf_op jit(solution)/shard_map/sweep/pallas_call | solution.py:395
  45.9 0.0 copy-done.2
  45.9 0.0 copy-start
  45.9 2.7 %copy-done = bf16[5,72,64,128]{3,2,1,0:T(8,128)(2,1)S(1)} copy-done((bf16[5,72,64,128]{3,2,1,0:T(8,128)(2,1)S(1)}, bf16[5,72,64,128]{3,2,1,0:T(8,128)(2,1)}, u32[]{:S(2)}) %copy-start) | copy-done | bytes 5898264
  48.6 5.7 %finish.1 = bf16[5,72,64,128]{3,2,1,0:T(8,128)(2,1)} custom-call(bf16[5,72,64,128]{3,2,1,0:T(8,128)(2,1)S(1)} %copy-done, f32[8,12,16,128]{3,2,1,0:T(8,128)S(1)} %sweep.1.inc_ref, bf16[256,512]{1,0:T(8,128)(2,1)S(1)} %copy-done.2), custom_call_target="tpu_custom_call" | custom-call | tf_op jit(solution)/shard_map/finish/pallas_call | solution.py:423
  (2 shorter events, 0.0 us)
Async XLA Ops:
  0.2 3.7 %copy-start.3 = (bf16[256,256]{1,0:T(8,128)(2,1)S(1)}, bf16[256,256]{1,0:T(8,128)(2,1)}, u32[]{:S(2)}) copy-start(bf16[256,256]{1,0:T(8,128)(2,1)} %constant.47.clone.wave_low_ref) | copy-start | bytes 393220
  0.2 3.7 %copy-start.4 = (bf16[256,256]{1,0:T(8,128)(2,1)S(1)}, bf16[256,256]{1,0:T(8,128)(2,1)}, u32[]{:S(2)}) copy-start(bf16[256,256]{1,0:T(8,128)(2,1)} %constant.46.clone.wave_high_ref) | copy-start | bytes 393220
  3.9 1.5 %copy-start.1 = (f32[72,3,16,128]{3,2,1,0:T(8,128)S(1)}, f32[72,3,16,128]{3,2,1,0:T(8,128)}, u32[]{:S(2)}) copy-start(f32[72,3,16,128]{3,2,1,0:T(8,128)} %pack.1) | copy-start | bytes 5308420
  5.4 40.5 %copy-start.2 = (bf16[256,512]{1,0:T(8,128)(2,1)S(1)}, bf16[256,512]{1,0:T(8,128)(2,1)}, u32[]{:S(2)}) copy-start(bf16[256,512]{1,0:T(8,128)(2,1)} %constant.45.clone.spread_ref) | copy-start | bytes 786436
  45.9 2.7 %copy-start = (bf16[5,72,64,128]{3,2,1,0:T(8,128)(2,1)S(1)}, bf16[5,72,64,128]{3,2,1,0:T(8,128)(2,1)}, u32[]{:S(2)}) copy-start(bf16[5,72,64,128]{3,2,1,0:T(8,128)(2,1)} %traj_ref.3) | copy-start | bytes 17694724
